TPU v7x, 32 devices: a whole 2x2x4 slice. The times are simulated.
32 devices in a mesh: seq: 8 (over y, x, core), fsdp: 4 (over z).
Axes of the slice: x: 2, y: 2, z: 4, core: 2. Of those that a mesh axis runs over, the one named last changes fastest.
Arguments:
- inputs: bfloat16 [4, 4096, 1280], P('fsdp', 'seq'), may hold values from -6 to 6
- w_query: float32 [1280, 1280], P(('seq', 'fsdp')), may hold values from -0.15625 to 0.15625
- w_key: float32 [1280, 1280], P(('seq', 'fsdp')), may hold values from -0.15625 to 0.15625
- w_value: float32 [1280, 1280], P(('seq', 'fsdp')), may hold values from -0.15625 to 0.15625
- w_proj: float32 [1280, 1280], P(('seq', 'fsdp')), may hold values from -1 to 1
- w_up: float32 [1280, 1280], P(('seq', 'fsdp')), may hold values from -0.15625 to 0.15625
- w_down: float32 [1280, 1280], P(('seq', 'fsdp')), may hold values from -0.3125 to 0.3125
- gain_first: float32 [1280], P(('seq', 'fsdp')), may hold values from 0.25 to 1.75
- gain_second: float32 [1280], P(('seq', 'fsdp')), may hold values from 0.25 to 1.75
- bias_up: float32 [1280], P(('seq', 'fsdp')), may hold values from -3 to 3
- bias_down: float32 [1280], P(('seq', 'fsdp')), may hold values from -3 to 3
- query_scale: float32 [80], replicated, may hold values from 0 to 2
- cotangent: bfloat16 [4, 4096, 1280], P('fsdp', 'seq'), may hold values from -6 to 6
Outputs:
- result: bfloat16 [4, 4096, 1280], P('fsdp', 'seq')
- grad_inputs: bfloat16 [4, 4096, 1280], P('fsdp', 'seq')
- grad_query: float32 [1280, 1280], P(('seq', 'fsdp'))
- grad_key: float32 [1280, 1280], P(('seq', 'fsdp'))
- grad_value: float32 [1280, 1280], P(('seq', 'fsdp'))
- grad_proj: float32 [1280, 1280], P(('seq', 'fsdp'))
- grad_up: float32 [1280, 1280], P(('seq', 'fsdp'))
- grad_down: float32 [1280, 1280], P(('seq', 'fsdp'))
- grad_first: float32 [1280], P(('seq', 'fsdp'))
- grad_second: float32 [1280], P(('seq', 'fsdp'))
- grad_bias_up: float32 [1280], P(('seq', 'fsdp'))
- grad_bias_down: float32 [1280], P(('seq', 'fsdp'))
- grad_scale: float32 [80], replicated
All inputs are finite; a program needn't handle non-finite values.
Results may differ from a plain program's by a relative error of at most 0.015.
The roundings to bfloat16 on the way count: a program that leaves them out, or rounds other values in their place, can miss the bound.
Values may be sent and summed in bfloat16 or wider, within the bound.
A program may use at most 192 MiB of HBM per device.

v0:
```python
import math

import jax
import jax.numpy as jnp
from jax import lax
from jax.sharding import PartitionSpec as P

H = 16
HD = 80


eps_norm = 1e-06
log_two_inverse = 1.442695


def rms_scale(values, gain):
    return values * lax.rsqrt(jnp.mean(values * values, axis=-1, keepdims=True) + eps_norm) * gain


def block_scores(query_block, key_rows, first_row, rows_block, length):
    scores = jnp.einsum(
        "bhdq,bhdk->bhqk", query_block, key_rows, preferred_element_type=jnp.float32
    )
    query_pos = first_row + lax.iota(jnp.int32, rows_block)
    key_pos = lax.iota(jnp.int32, length)
    allowed = key_pos[None, :] <= query_pos[:, None]
    return (scores, allowed)


def head_forward(queries, key_rows, value_rows):
    batches, head_count, depth, length = queries.shape
    rows_block = min(512, length)
    blocks = length // rows_block

    def advance(block_index, state_pair):
        mixed_out, logsum = state_pair
        first_row = block_index * rows_block
        query_block = lax.dynamic_slice_in_dim(queries, first_row, rows_block, 3)
        scores, allowed = block_scores(query_block, key_rows, first_row, rows_block, length)
        scores = jnp.where(allowed, scores, -1e30)
        row_max = jnp.max(scores, axis=-1, keepdims=True)
        shifted = jnp.exp(scores - row_max)
        exp_total = jnp.sum(shifted, axis=-1, keepdims=True)
        probs_low = (shifted / exp_total).astype(jnp.bfloat16)
        block_out = jnp.einsum(
            "bhqk,bhdk->bhdq", probs_low, value_rows, preferred_element_type=jnp.float32
        )
        mixed_out = lax.dynamic_update_slice_in_dim(
            mixed_out, block_out.astype(jnp.bfloat16), first_row, 3
        )
        block_lse = (row_max + jnp.log(exp_total))[..., 0]
        logsum = lax.dynamic_update_slice_in_dim(logsum, block_lse, first_row, 2)
        return (mixed_out, logsum)

    start_pair = (
        jnp.zeros(queries.shape, jnp.bfloat16),
        jnp.zeros((batches, head_count, length), jnp.float32),
    )
    return lax.fori_loop(0, blocks, advance, start_pair)


def head_backward(queries, key_rows, value_rows, logsum, grad_mixed):
    batches, head_count, depth, length = queries.shape
    rows_block = min(512, length)
    blocks = length // rows_block

    def advance(block_index, state_triple):
        grad_queries, grad_keys, grad_values = state_triple
        first_row = block_index * rows_block
        query_block = lax.dynamic_slice_in_dim(queries, first_row, rows_block, 3)
        grad_block = lax.dynamic_slice_in_dim(grad_mixed, first_row, rows_block, 3)
        lse_block = lax.dynamic_slice_in_dim(logsum, first_row, rows_block, 2)
        scores, allowed = block_scores(query_block, key_rows, first_row, rows_block, length)
        probs = jnp.where(allowed, jnp.exp(scores - lse_block[..., None]), 0.0)
        probs_low = probs.astype(jnp.bfloat16)
        grad_probs = jnp.einsum(
            "bhdq,bhdk->bhqk", grad_block, value_rows, preferred_element_type=jnp.float32
        )
        delta = jnp.sum(probs * grad_probs, axis=-1, keepdims=True)
        grad_scores = (probs * (grad_probs - delta)).astype(jnp.bfloat16)
        query_part = jnp.einsum(
            "bhqk,bhdk->bhdq", grad_scores, key_rows, preferred_element_type=jnp.float32
        )
        grad_queries = lax.dynamic_update_slice_in_dim(
            grad_queries, query_part.astype(jnp.bfloat16), first_row, 3
        )
        grad_keys = grad_keys + jnp.einsum(
            "bhqk,bhdq->bhdk", grad_scores, query_block, preferred_element_type=jnp.float32
        )
        grad_values = grad_values + jnp.einsum(
            "bhqk,bhdq->bhdk", probs_low, grad_block, preferred_element_type=jnp.float32
        )
        return (grad_queries, grad_keys, grad_values)

    start_triple = (
        jnp.zeros(queries.shape, jnp.bfloat16),
        jnp.zeros(queries.shape, jnp.float32),
        jnp.zeros(queries.shape, jnp.float32),
    )
    grad_queries, grad_keys, grad_values = lax.fori_loop(0, blocks, advance, start_triple)
    return (grad_queries, grad_keys.astype(jnp.bfloat16), grad_values.astype(jnp.bfloat16))


def body(
    inputs,
    w_query,
    w_key,
    w_value,
    w_proj,
    w_up,
    w_down,
    gain_first,
    gain_second,
    bias_up,
    bias_down,
    query_scale,
    cotangent,
):
    groups = lax.axis_size("seq")
    batches = inputs.shape[0]
    head_count = H // groups
    bf = jnp.bfloat16
    params = (
        lax.all_gather(w_query.astype(bf), ("seq", "fsdp"), axis=0, tiled=True),
        lax.all_gather(w_key.astype(bf), ("seq", "fsdp"), axis=0, tiled=True),
        lax.all_gather(w_value.astype(bf), ("seq", "fsdp"), axis=0, tiled=True),
        lax.all_gather(w_proj.astype(bf), ("seq", "fsdp"), axis=0, tiled=True),
        lax.all_gather(w_up.astype(bf), ("seq", "fsdp"), axis=0, tiled=True),
        lax.all_gather(w_down.astype(bf), ("seq", "fsdp"), axis=0, tiled=True),
        lax.all_gather(gain_first.astype(bf), ("seq", "fsdp"), axis=0, tiled=True),
        lax.all_gather(gain_second.astype(bf), ("seq", "fsdp"), axis=0, tiled=True),
        lax.all_gather(bias_up.astype(bf), ("seq", "fsdp"), axis=0, tiled=True),
        lax.all_gather(bias_down.astype(bf), ("seq", "fsdp"), axis=0, tiled=True),
    )
    query_w, key_w, value_w, proj_w, up_w, down_w, first_gain, second_gain, upbias, downbias = (
        params
    )
    first_gain = first_gain.astype(jnp.float32)
    second_gain = second_gain.astype(jnp.float32)
    scale_dims = jax.nn.softplus(query_scale) * log_two_inverse / math.sqrt(HD)
    tiled_scale = jnp.tile(scale_dims, H)
    float_in = inputs.astype(jnp.float32)
    normed = rms_scale(float_in, first_gain).astype(bf)
    query_full = jnp.einsum("btd,de->bet", normed, query_w, preferred_element_type=jnp.float32)
    query_low = (query_full * tiled_scale[:, None]).astype(bf)
    key_low = jnp.einsum("btd,de->bet", normed, key_w, preferred_element_type=jnp.float32).astype(
        bf
    )
    value_low = jnp.einsum(
        "btd,de->bet", normed, value_w, preferred_element_type=jnp.float32
    ).astype(bf)
    query_heads, key_heads, value_heads = (
        lax.all_to_all(query_low, "seq", split_axis=1, concat_axis=2, tiled=True),
        lax.all_to_all(key_low, "seq", split_axis=1, concat_axis=2, tiled=True),
        lax.all_to_all(value_low, "seq", split_axis=1, concat_axis=2, tiled=True),
    )
    length = query_heads.shape[2]
    head_shape = (batches, head_count, HD, length)
    query_heads = query_heads.reshape(head_shape)
    key_heads = key_heads.reshape(head_shape)
    value_heads = value_heads.reshape(head_shape)
    mixed_heads, logsum = head_forward(query_heads, key_heads, value_heads)
    mixed = lax.all_to_all(
        mixed_heads.reshape(batches, head_count * HD, length),
        "seq",
        split_axis=2,
        concat_axis=1,
        tiled=True,
    )
    middle = float_in + jnp.einsum("bdt,de->bte", mixed, proj_w, preferred_element_type=jnp.float32)
    second = rms_scale(middle, second_gain).astype(bf)
    hidden = jnp.dot(second, up_w, preferred_element_type=jnp.float32) + upbias.astype(jnp.float32)
    active = jax.nn.silu(hidden).astype(bf)
    result = (
        middle
        + jnp.dot(active, down_w, preferred_element_type=jnp.float32)
        + downbias.astype(jnp.float32)
    )
    params = (
        lax.all_gather(w_query.astype(bf), ("seq", "fsdp"), axis=0, tiled=True),
        lax.all_gather(w_key.astype(bf), ("seq", "fsdp"), axis=0, tiled=True),
        lax.all_gather(w_value.astype(bf), ("seq", "fsdp"), axis=0, tiled=True),
        lax.all_gather(w_proj.astype(bf), ("seq", "fsdp"), axis=0, tiled=True),
        lax.all_gather(w_up.astype(bf), ("seq", "fsdp"), axis=0, tiled=True),
        lax.all_gather(w_down.astype(bf), ("seq", "fsdp"), axis=0, tiled=True),
        lax.all_gather(gain_first.astype(bf), ("seq", "fsdp"), axis=0, tiled=True),
        lax.all_gather(gain_second.astype(bf), ("seq", "fsdp"), axis=0, tiled=True),
        lax.all_gather(bias_up.astype(bf), ("seq", "fsdp"), axis=0, tiled=True),
        lax.all_gather(bias_down.astype(bf), ("seq", "fsdp"), axis=0, tiled=True),
    )
    query_w, key_w, value_w, proj_w, up_w, down_w, first_again, second_again, upbias, downbias = (
        params
    )
    grad_top = cotangent.astype(jnp.float32)
    grad_bdown = jnp.sum(grad_top, axis=(0, 1))
    top_low = grad_top.astype(bf)
    grad_wdown = jnp.einsum("btf,btd->fd", active, top_low, preferred_element_type=jnp.float32)
    grad_active = jnp.einsum("btd,fd->btf", top_low, down_w, preferred_element_type=jnp.float32)
    unused_silu, silu_pull = jax.vjp(jax.nn.silu, hidden)
    grad_hidden = silu_pull(grad_active)[0]
    grad_bup = jnp.sum(grad_hidden, axis=(0, 1))
    hidden_low = grad_hidden.astype(bf)
    grad_wup = jnp.einsum("btd,btf->df", second, hidden_low, preferred_element_type=jnp.float32)
    grad_second_in = jnp.einsum("btf,df->btd", hidden_low, up_w, preferred_element_type=jnp.float32)
    unused_second, second_pull = jax.vjp(rms_scale, middle, second_gain)
    grad_middle, grad_gsecond = second_pull(grad_second_in)
    mlp_owned = (
        lax.psum_scatter(grad_wup, ("seq", "fsdp"), scatter_dimension=0, tiled=True),
        lax.psum_scatter(grad_wdown, ("seq", "fsdp"), scatter_dimension=0, tiled=True),
        lax.psum_scatter(grad_gsecond, ("seq", "fsdp"), scatter_dimension=0, tiled=True),
        lax.psum_scatter(grad_bup, ("seq", "fsdp"), scatter_dimension=0, tiled=True),
        lax.psum_scatter(grad_bdown, ("seq", "fsdp"), scatter_dimension=0, tiled=True),
    )
    grad_middle = grad_middle + grad_top
    middle_low = grad_middle.astype(bf)
    grad_wproj = jnp.einsum("bdt,bte->de", mixed, middle_low, preferred_element_type=jnp.float32)
    proj_owned = lax.psum_scatter(grad_wproj, ("seq", "fsdp"), scatter_dimension=0, tiled=True)
    grad_mixed = jnp.einsum(
        "bte,de->bdt", middle_low, proj_w, preferred_element_type=jnp.float32
    ).astype(bf)
    grad_mixed_heads = lax.all_to_all(grad_mixed, "seq", split_axis=1, concat_axis=2, tiled=True)
    grad_qheads, grad_kheads, grad_vheads = head_backward(
        query_heads, key_heads, value_heads, logsum, grad_mixed_heads.reshape(head_shape)
    )
    flat_shape = (batches, head_count * HD, length)
    grad_scaled, grad_keyrows, grad_valrows = (
        lax.all_to_all(
            grad_qheads.reshape(flat_shape), "seq", split_axis=2, concat_axis=1, tiled=True
        ),
        lax.all_to_all(
            grad_kheads.reshape(flat_shape), "seq", split_axis=2, concat_axis=1, tiled=True
        ),
        lax.all_to_all(
            grad_vheads.reshape(flat_shape), "seq", split_axis=2, concat_axis=1, tiled=True
        ),
    )
    scaled_float = grad_scaled.astype(jnp.float32)
    query_grad = (scaled_float * tiled_scale[:, None]).astype(bf)
    scale_partial = jnp.sum(jnp.sum(scaled_float * query_full, axis=(0, 2)).reshape(H, HD), axis=0)
    grad_wquery = jnp.einsum("btd,bet->de", normed, query_grad, preferred_element_type=jnp.float32)
    grad_wkey = jnp.einsum("btd,bet->de", normed, grad_keyrows, preferred_element_type=jnp.float32)
    grad_wvalue = jnp.einsum(
        "btd,bet->de", normed, grad_valrows, preferred_element_type=jnp.float32
    )
    grad_first_in = jnp.einsum(
        "bet,de->btd", query_grad, query_w, preferred_element_type=jnp.float32
    )
    grad_first_in = grad_first_in + jnp.einsum(
        "bet,de->btd", grad_keyrows, key_w, preferred_element_type=jnp.float32
    )
    grad_first_in = grad_first_in + jnp.einsum(
        "bet,de->btd", grad_valrows, value_w, preferred_element_type=jnp.float32
    )
    unused_first, first_pull = jax.vjp(rms_scale, float_in, first_gain)
    grad_below, grad_gfirst = first_pull(grad_first_in)
    grad_inputs = (grad_middle + grad_below).astype(bf)
    attn_owned = (
        lax.psum_scatter(grad_wquery, ("seq", "fsdp"), scatter_dimension=0, tiled=True),
        lax.psum_scatter(grad_wkey, ("seq", "fsdp"), scatter_dimension=0, tiled=True),
        lax.psum_scatter(grad_wvalue, ("seq", "fsdp"), scatter_dimension=0, tiled=True),
        lax.psum_scatter(grad_gfirst, ("seq", "fsdp"), scatter_dimension=0, tiled=True),
    )
    reduced = (
        attn_owned[0],
        attn_owned[1],
        attn_owned[2],
        proj_owned,
        mlp_owned[0],
        mlp_owned[1],
        attn_owned[3],
        mlp_owned[2],
        mlp_owned[3],
        mlp_owned[4],
    )
    scale_total = lax.psum(scale_partial, ("seq", "fsdp"))
    grad_scale = scale_total * jax.nn.sigmoid(query_scale) * log_two_inverse / math.sqrt(HD)
    return (
        result.astype(bf),
        grad_inputs,
        reduced[0],
        reduced[1],
        reduced[2],
        reduced[3],
        reduced[4],
        reduced[5],
        reduced[6],
        reduced[7],
        reduced[8],
        reduced[9],
        grad_scale,
    )


def solution(mesh):
    return jax.shard_map(
        body,
        mesh=mesh,
        in_specs=(
            P("fsdp", "seq", None),
            P(("seq", "fsdp"), None),
            P(("seq", "fsdp"), None),
            P(("seq", "fsdp"), None),
            P(("seq", "fsdp"), None),
            P(("seq", "fsdp"), None),
            P(("seq", "fsdp"), None),
            P(("seq", "fsdp")),
            P(("seq", "fsdp")),
            P(("seq", "fsdp")),
            P(("seq", "fsdp")),
            P(),
            P("fsdp", "seq", None),
        ),
        out_specs=(
            P("fsdp", "seq", None),
            P("fsdp", "seq", None),
            P(("seq", "fsdp"), None),
            P(("seq", "fsdp"), None),
            P(("seq", "fsdp"), None),
            P(("seq", "fsdp"), None),
            P(("seq", "fsdp"), None),
            P(("seq", "fsdp"), None),
            P(("seq", "fsdp")),
            P(("seq", "fsdp")),
            P(("seq", "fsdp")),
            P(("seq", "fsdp")),
            P(),
        ),
        check_vma=False,
    )
```

profile of v0, /device:TPU:0, one launch (start us, length us, event | category | flops | bytes accessed | tf_op | source)
XLA Modules:
  0.0 1580.5 jit_solution(6925407331183194057)
XLA Ops:
  19.1 42.3 %all-reduce.9 = (bf16[1280]{0:T(1024)(128)(2,1)S(1)}, bf16[1280]{0:T(1024)(128)(2,1)}, bf16[1280]{0:T(1024)(128)(2,1)}, bf16[1280]{0:T(1024)(128)(2,1)}) all-reduce(bf16[1280]{0:T(1024)(128)(2,1)S(1)} %dynamic-update-slice, bf16[1280]{0:T(1024)(128)(2,1)S(1)} %dynamic-update-slice.3, ...), channel_id=1, replica_groups=mesh['seq'=8,'fsdp'=4] {'seq','fsdp'}, use_global_device_ids=true, to_apply=%add | all-reduce | flops 5120 | bytes 20480
  99.6 38.1 %all-gather.9.cloned.1.call-done = bf16[1280,1280]{1,0:T(8,128)(2,1)} async-done(((bf16[40,1280]{1,0:T(8,128)(2,1)}), bf16[1280,1280]{1,0:T(8,128)(2,1)}) %all-gather.9.cloned.1.call-update) | async-done | bytes 3276816 | tf_op jit(solution)/shard_map/all_gather | solution.py:125
  161.9 39.7 %all-gather.11.cloned.1.call-done = bf16[1280,1280]{1,0:T(8,128)(2,1)} async-done(((bf16[40,1280]{1,0:T(8,128)(2,1)}), bf16[1280,1280]{1,0:T(8,128)(2,1)}) %all-gather.11.cloned.1.call-update) | async-done | bytes 3276816 | tf_op jit(solution)/shard_map/all_gather | solution.py:126
  259.6 131.9 %while.33 = (s32[]{:T(128)}, bf16[1,2,80,4096]{3,2,1,0:T(8,128)(2,1)S(1)}, f32[1,2,4096]{2,1,0:T(2,128)S(1)}, bf16[1,2,80,4096]{3,2,1,0:T(8,128)(2,1)}, bf16[1,2...) while((s32[]{:T(128)}, ...), condition=%wide.region_4.5_spmd, body=%wide.region_1.4_spmd.sunk | while | flops 1382104576 | bytes 61706408 | solution.py:59
  399.9 23.9 %reduce.25 = bf16[4096,160]{1,0:T(8,128)(2,1)S(1)} reduce(bf16[4096,1,160]{2,1,0:T(2,128)(2,1)} %bitcast.285, bf16[]{:T(256)} %broadcast.204), dimensions={1}, to_apply=%bitcast.198.reduce_sub_computation | reduce | bytes 2621442
  431.4 18.1 %all-to-all-done.3 = bf16[8,2,40960]{2,1,0:T(2,128)(2,1)S(1)} async-done(((bf16[8,2,40960]{2,1,0:T(2,128)(2,1)}), bf16[8,2,40960]{2,1,0:T(2,128)(2,1)S(1)}, u32[]{:S(2)}, u32[]{:S(2)}) %all-to-all-start.3) | async-done | bytes 1310752 | tf_op jit(solution)/shard_map/all_to_all | solution.py:163
  533.0 15.3 all-to-all-done.4
  557.6 451.0 %while.34 = (s32[]{:T(128)}, bf16[1,2,80,4096]{3,2,1,0:T(8,128)(2,1)}, f32[1,2,80,4096]{3,2,1,0:T(8,128)}, f32[1,2,80,4096]{3,2,1,0:T(8,128)}, bf16[1,2,80,4096]...) while((s32[]{:T(128)}, ...), condition=%wide.region_9.10_spmd.clone, body=%wide.region_7.9_spmd.clone.sunk | while | flops 3410574848 | bytes 204013840 | solution.py:100
  568.4 12.7 multiply_reduce_fusion.4
  624.1 12.7 multiply_reduce_fusion.4
  680.6 12.7 multiply_reduce_fusion.4
  737.0 12.7 multiply_reduce_fusion.4
  850.0 12.7 multiply_reduce_fusion.4
  906.5 12.7 multiply_reduce_fusion.4
  963.0 12.7 multiply_reduce_fusion.4
  1018.4 23.6 %reduce.27 = bf16[4096,160]{1,0:T(8,128)(2,1)S(1)} reduce(bf16[4096,1,160]{2,1,0:T(2,128)(2,1)} %bitcast.287, bf16[]{:T(256)} %broadcast.204), dimensions={1}, to_apply=%bitcast.202.reduce_sub_computation | reduce | bytes 2621442
  1045.3 20.6 %all_to_all.114 = bf16[8,2,40960]{2,1,0:T(2,128)(2,1)S(1)} all-to-all(bf16[8,2,40960]{2,1,0:T(2,128)(2,1)S(1)} %reshape.481), channel_id=1, replica_groups=mesh['seq'=8,'fsdp'=4] {'seq'}, dimensions={0} | all-to-all | bytes 2621440 | tf_op jit(solution)/shard_map/all_to_all | solution.py:227
  1103.0 23.6 %reduce.28 = bf16[4096,160]{1,0:T(8,128)(2,1)S(1)} reduce(bf16[4096,1,160]{2,1,0:T(2,128)(2,1)} %bitcast.289, bf16[]{:T(256)} %broadcast.204), dimensions={1}, to_apply=%bitcast.204.reduce_sub_computation | reduce | bytes 2621442
  1129.9 24.7 %all_to_all.115 = bf16[8,2,40960]{2,1,0:T(2,128)(2,1)S(1)} all-to-all(bf16[8,2,40960]{2,1,0:T(2,128)(2,1)S(1)} %reshape.483), channel_id=1, replica_groups=mesh['seq'=8,'fsdp'=4] {'seq'}, dimensions={0} | all-to-all | bytes 2621440 | tf_op jit(solution)/shard_map/all_to_all | solution.py:230
  1186.9 23.6 %reduce.29 = bf16[4096,160]{1,0:T(8,128)(2,1)S(1)} reduce(bf16[4096,1,160]{2,1,0:T(2,128)(2,1)} %bitcast.284, bf16[]{:T(256)} %broadcast.204), dimensions={1}, to_apply=%bitcast.206.reduce_sub_computation | reduce | bytes 2621442
  1214.5 25.9 %all_to_all.116 = bf16[8,2,40960]{2,1,0:T(2,128)(2,1)S(1)} all-to-all(bf16[8,2,40960]{2,1,0:T(2,128)(2,1)} %reshape.485), channel_id=1, replica_groups=mesh['seq'=8,'fsdp'=4] {'seq'}, dimensions={0} | all-to-all | bytes 2621440 | tf_op jit(solution)/shard_map/all_to_all | solution.py:233
  1287.0 40.8 %all-reduce.8 = (f32[1280]{0:T(1024)S(1)}, f32[1280]{0:T(1024)S(1)}, f32[1280]{0:T(1024)S(1)}, f32[1280]{0:T(1024)S(1)}, f32[80]{0:T(128)S(1)}) all-reduce(f32[1280]{0:T(1024)S(1)} %get-tuple-element.316, f32[1280]{0:T(1024)S(1)} %copy-done.34, f32[1280]{0:T(1024)S(1)} %copy-done.33, ...), channel_id=8, replica_groups=mesh['seq'=8,'fsdp'=4] {'seq','fsdp'}, use_global_device_ids=true, to_apply=%region_18.19.clone | all-reduce | flops 5200 | bytes 41600
  1335.1 76.7 %reduce-scatter.9.cloned.1.call-done = f32[40,1280]{1,0:T(8,128)} async-done(((f32[1280,1280]{1,0:T(8,128)}), f32[40,1280]{1,0:T(8,128)}) %reduce-scatter.9.cloned.1.call-update) | async-done | bytes 204816 | tf_op jit(solution)/shard_map/reduce_scatter | solution.py:259
  1411.8 161.6 %reduce-scatter.11.cloned.1.call-done = f32[40,1280]{1,0:T(8,128)} async-done(((f32[1280,1280]{1,0:T(8,128)}), f32[40,1280]{1,0:T(8,128)}) %reduce-scatter.11.cloned.1.call-update) | async-done | bytes 204816 | tf_op jit(solution)/shard_map/reduce_scatter | solution.py:260
  (403 shorter events, 876.7 us)
Async XLA Ops:
  7.2 54.9 %copy-start.4 = (bf16[1,512,1280]{2,1,0:T(8,128)(2,1)S(1)}, bf16[1,512,1280]{2,1,0:T(8,128)(2,1)}, u32[]{:S(2)}) copy-start(bf16[1,512,1280]{2,1,0:T(8,128)(2,1)} %param.17) | copy-start | bytes 3932164
  7.2 66.5 %all-gather.7.cloned.1.call-start = ((), (), s32[]{:S(2)}) async-start(), calls=%async_computation.14 | async-start | bytes 3379200 | tf_op jit(solution)/shard_map/all_gather | solution.py:124
  8.9 128.8 %all-gather.9.cloned.1.call-start = ((), (), s32[]{:S(2)}) async-start(), calls=%async_computation.15 | async-start | bytes 3379200 | tf_op jit(solution)/shard_map/all_gather | solution.py:125
  10.6 191.0 %all-gather.11.cloned.1.call-start = ((), (), s32[]{:S(2)}) async-start(), calls=%async_computation.16 | async-start | bytes 3379200 | tf_op jit(solution)/shard_map/all_gather | solution.py:126
  12.3 454.2 %all-gather.13.cloned.1.call-start = ((), (), s32[]{:S(2)}) async-start(), calls=%async_computation.17 | async-start | bytes 3379200 | tf_op jit(solution)/shard_map/all_gather | solution.py:127
  13.9 458.4 %all-gather.15.cloned.1.call-start = ((), (), s32[]{:S(2)}) async-start(), calls=%async_computation.18 | async-start | bytes 3379200 | tf_op jit(solution)/shard_map/all_gather | solution.py:128
  61.4 140.2 %copy-start.24 = (f32[1280]{0:T(1024)}, f32[1280]{0:T(1024)S(1)}, u32[]{:S(2)}) copy-start(f32[1280]{0:T(1024)S(1)} %convert_element_type.229) | copy-start | bytes 15364
  62.1 15.4 copy-start.26
  62.5 11.2 copy-start.31
  62.5 139.1 %copy-start.29 = (f32[512]{0:T(512)}, f32[512]{0:T(512)S(1)}, u32[]{:S(2)}) copy-start(f32[512]{0:T(512)S(1)} %fusion.101) | copy-start | bytes 6148
  95.3 61.8 %all-to-all-start = ((bf16[8,2,40960]{2,1,0:T(2,128)(2,1)}), bf16[8,2,40960]{2,1,0:T(2,128)(2,1)}, u32[]{:S(2)}, u32[]{:S(2)}) async-start(bf16[8,2,40960]{2,1,0:T(2,128)(2,1)} %reshape.471), calls=%async_computation | async-start | bytes 2621440 | tf_op jit(solution)/shard_map/all_to_all | solution.py:153
  157.1 69.1 %all-to-all-start.1 = ((bf16[8,2,40960]{2,1,0:T(2,128)(2,1)}), bf16[8,2,40960]{2,1,0:T(2,128)(2,1)}, u32[]{:S(2)}, u32[]{:S(2)}) async-start(bf16[8,2,40960]{2,1,0:T(2,128)(2,1)} %reshape.473), calls=%async_computation.1 | async-start | bytes 2621440 | tf_op jit(solution)/shard_map/all_to_all | solution.py:154
  226.2 22.9 %all-to-all-start.2 = ((bf16[8,2,40960]{2,1,0:T(2,128)(2,1)}), bf16[8,2,40960]{2,1,0:T(2,128)(2,1)}, u32[]{:S(2)}, u32[]{:S(2)}) async-start(bf16[8,2,40960]{2,1,0:T(2,128)(2,1)} %reshape.475), calls=%async_computation.2 | async-start | bytes 2621440 | tf_op jit(solution)/shard_map/all_to_all | solution.py:155
  230.5 248.1 %all-gather.17.cloned.1.call-start = ((), (), s32[]{:S(2)}) async-start(), calls=%async_computation.19 | async-start | bytes 3379200 | tf_op jit(solution)/shard_map/all_gather | solution.py:129
  427.8 21.7 %all-to-all-start.3 = ((bf16[8,2,40960]{2,1,0:T(2,128)(2,1)}), bf16[8,2,40960]{2,1,0:T(2,128)(2,1)S(1)}, u32[]{:S(2)}, u32[]{:S(2)}) async-start(bf16[8,2,40960]{2,1,0:T(2,128)(2,1)} %reshape.477), calls=%async_computation.3 | async-start | bytes 2621440 | tf_op jit(solution)/shard_map/all_to_all | solution.py:163
  431.3 903.7 %reduce-scatter.13.cloned.1.call-start = ((), (), s32[]{:S(2)}) async-start(), calls=%async_computation.23 | async-start | bytes 6758400 | tf_op jit(solution)/shard_map/reduce_scatter | solution.py:217
  494.6 840.5 %reduce-scatter.15.cloned.1.call-start = ((), (), s32[]{:S(2)}) async-start(), calls=%async_computation.24 | async-start | bytes 6758400 | tf_op jit(solution)/shard_map/reduce_scatter | solution.py:208
  522.6 25.8 %all-to-all-start.4 = ((bf16[8,2,40960]{2,1,0:T(2,128)(2,1)}), bf16[8,2,40960]{2,1,0:T(2,128)(2,1)S(1)}, u32[]{:S(2)}, u32[]{:S(2)}) async-start(bf16[8,2,40960]{2,1,0:T(2,128)(2,1)} %reshape.479), calls=%async_computation.4 | async-start | bytes 2621440 | tf_op jit(solution)/shard_map/all_to_all | solution.py:221
  526.1 809.0 %reduce-scatter.17.cloned.1.call-start = ((), (), s32[]{:S(2)}) async-start(), calls=%async_computation.25 | async-start | bytes 6758400 | tf_op jit(solution)/shard_map/reduce_scatter | solution.py:209
  533.0 802.1 %reduce-scatter.7.cloned.1.call-start = ((), (), s32[]{:S(2)}) async-start(), calls=%async_computation.20 | async-start | bytes 6758400 | tf_op jit(solution)/shard_map/reduce_scatter | solution.py:258
  1089.8 322.0 %reduce-scatter.9.cloned.1.call-start = ((), (), s32[]{:S(2)}) async-start(), calls=%async_computation.21 | async-start | bytes 6758400 | tf_op jit(solution)/shard_map/reduce_scatter | solution.py:259
  1176.5 397.0 %reduce-scatter.11.cloned.1.call-start = ((), (), s32[]{:S(2)}) async-start(), calls=%async_computation.22 | async-start | bytes 6758400 | tf_op jit(solution)/shard_map/reduce_scatter | solution.py:260
  1283.1 47.1 %copy-start.41 = (f32[80]{0:T(128)S(1)}, f32[80]{0:T(128)}, u32[]{:S(2)}) copy-start(f32[80]{0:T(128)} %param.28) | copy-start | bytes 964
  1283.1 47.6 %copy-start.32 = (f32[512]{0:T(512)S(1)}, f32[512]{0:T(512)}, u32[]{:S(2)}) copy-start(f32[512]{0:T(512)} %copy-done.31) | copy-start | bytes 6148
  (56 other events, 205.7 us)
Sparse Core Ops, SparseCore 0:
  11.4 62.2 all-gather.6
  77.1 60.6 all-gather.8
  141.2 60.4 all-gather.10
  204.9 59.2 all-gather.12
  267.4 58.3 all-gather.14
  329.1 58.2 all-gather.16
  494.7 159.0 reduce-scatter.12
  656.6 159.0 reduce-scatter.14
  818.6 159.3 reduce-scatter.16
  1090.0 160.2 reduce-scatter.6
  1253.1 158.6 reduce-scatter.8
  1414.6 158.8 reduce-scatter.10
where the time goes:
time: 1590 us; the launch traced here: 1580 us
  matrix products  496 us (31%)
  waiting for transfers between devices  366 us (23%)
  other arithmetic  316 us (20%)
  local copies, waits for them, and re-layouts  211 us (13%)
  blocking collectives  154 us (10%)
  starting transfers between devices  21.4 us (1%)
    reduce_scatter x1, waiting for transfers between devices, body(): lax.psum_scatter(grad_wvalue, ('seq', 'fsdp'), scatter_dimension=0, tiled...  162 us
    unnamed x10, other arithmetic  133 us
    dot_general x16, matrix products, block_scores(): jnp.einsum('bhdq,bhdk->bhqk', query_block, key_rows, preferred_element_ty...  104 us
    dot_general x8, matrix products, advance(): jnp.einsum('bhdq,bhdk->bhqk', grad_block, value_rows, preferred_element_t...  101 us
    convert_element_type x8, other arithmetic, advance(): grad_scores = (probs * (grad_probs - delta)).astype(jnp.bfloat16)  99.3 us
    unnamed x115, local copies, waits for them, and re-layouts  86.7 us
    unnamed x2, blocking collectives  83.1 us
    reduce_scatter x1, waiting for transfers between devices, body(): lax.psum_scatter(grad_wkey, ('seq', 'fsdp'), scatter_dimension=0, tiled=T...  76.7 us
  transfers between devices with their start and end apart: 17, of which 8 were waited for; matrix products, arithmetic and copies ran while one was open for 62% of the time, Pallas kernels for 0%

commit v1 on v0

v1 whole, which is shorter than its diff:
```python
import functools
import math

import jax
import jax.numpy as jnp
from jax import lax
from jax.experimental import pallas as pl
from jax.experimental.pallas import tpu as pltpu
from jax.sharding import PartitionSpec as P

H = 16
HD = 80
eps_norm = 1e-06
log_two_inverse = 1.442695
bf = jnp.bfloat16
f32 = jnp.float32
NEG = -1e30


def rms_scale(values, gain):
    return values * lax.rsqrt(jnp.mean(values * values, axis=-1, keepdims=True) + eps_norm) * gain


def dot(a,b,ca=1,cb=0):
    return lax.dot_general(a,b,(((ca,),(cb,)),((),())),preferred_element_type=f32)

def fwd_kernel(BQ,BK,qt,k,vt,ot,lse):
    nh,hd,L=qt.shape
    i=pl.program_id(0)
    q=[qt[h,:,pl.ds(pl.multiple_of(i*BQ,BQ),BQ)] for h in range(nh)]
    def step(j,carry,diag=None):
        out=[]
        s=[]
        for h in range(nh):
            kk=k[h,pl.ds(pl.multiple_of(j*BK,BK),BK),:]
            s.append(dot(kk,q[h]))
        for h in range(nh):
            m,l,acc=carry[h]
            sh=s[h]
            if diag is not None:
                kp=lax.broadcasted_iota(jnp.int32,sh.shape,0)+diag*BK
                qp=lax.broadcasted_iota(jnp.int32,sh.shape,1)
                sh=jnp.where(kp<=qp,sh,NEG)
            mn=jnp.maximum(m,jnp.max(sh,axis=0,keepdims=True))
            a=jnp.exp(m-mn)
            p=jnp.exp(sh-mn)
            l=l*a+jnp.sum(p,axis=0,keepdims=True)
            vv=vt[h,:,pl.ds(pl.multiple_of(j*BK,BK),BK)]
            acc=acc*a+dot(vv,p.astype(bf))
            out.append((mn,l,acc))
        return tuple(out)
    init=tuple((jnp.full((1,BQ),NEG,f32),jnp.zeros((1,BQ),f32),jnp.zeros((hd,BQ),f32)) for _ in range(nh))
    r=BQ//BK
    c=lax.fori_loop(0,i*r,step,init)
    for d in range(r):
        c=step(i*r+d,c,d)
    for h in range(nh):
        m,l,acc=c[h]
        ot[h,:,:]=(acc/l).astype(bf)
        lse[h,:,:]=m+jnp.log(l)
def flash_fwd(qt,k,vt,BQ=512,BK=512):
    nh,hd,L=qt.shape
    return pl.pallas_call(functools.partial(fwd_kernel,BQ,BK),grid=(L//BQ,),
      in_specs=[pl.BlockSpec((nh,hd,L),lambda i:(0,0,0)),pl.BlockSpec((nh,L,hd),lambda i:(0,0,0)),pl.BlockSpec((nh,hd,L),lambda i:(0,0,0))],
      out_specs=[pl.BlockSpec((nh,hd,BQ),lambda i:(0,0,i)),pl.BlockSpec((nh,1,BQ),lambda i:(0,0,i))],
      out_shape=[jax.ShapeDtypeStruct((nh,hd,L),bf),jax.ShapeDtypeStruct((nh,1,L),f32)],
      compiler_params=pltpu.CompilerParams(vmem_limit_bytes=60<<20),name=f"fwd{BQ}_{BK}")(qt,k,vt)

def bwd_kernel(BQ,BK,qt,q,kt,k,v,dot_,do,lse,delta,dqt,dk,dv,dks,dvs):
    nh,hd,L=qt.shape
    i=pl.program_id(0); nb=L//BQ
    @pl.when(i==0)
    def _():
        dks[...]=jnp.zeros_like(dks); dvs[...]=jnp.zeros_like(dvs)
    qs=pl.ds(pl.multiple_of(i*BQ,BQ),BQ)
    def step(j,carry,diag=None):
        ks=pl.ds(pl.multiple_of(j*BK,BK),BK)
        s=[dot(k[h,ks,:],qt[h,:,qs]) for h in range(nh)]
        dp=[dot(v[h,ks,:],dot_[h,:,qs]) for h in range(nh)]
        out=[]
        for h in range(nh):
            p=jnp.exp(s[h]-lse[h,:,qs])
            if diag is not None:
                kp=lax.broadcasted_iota(jnp.int32,p.shape,0)+diag*BK
                qp=lax.broadcasted_iota(jnp.int32,p.shape,1)
                p=jnp.where(kp<=qp,p,0.0)
            ds=(p*(dp[h]-delta[h,:,qs])).astype(bf)
            dvs[h,ks,:]+=dot(p.astype(bf),do[h,qs,:])
            dks[h,ks,:]+=dot(ds,q[h,qs,:])
            out.append(carry[h]+dot(kt[h,:,ks],ds))
        return tuple(out)
    init=tuple(jnp.zeros((hd,BQ),f32) for _ in range(nh))
    r=BQ//BK
    c=lax.fori_loop(0,i*r,step,init)
    for d in range(r): c=step(i*r+d,c,d)
    for h in range(nh): dqt[h,:,:]=c[h].astype(bf)
    @pl.when(i==nb-1)
    def _():
        dk[...]=dks[...].astype(bf); dv[...]=dvs[...].astype(bf)
def flash_bwd(qt,q,kt,k,v,dot_,do,lse,delta,BQ=512,BK=512):
    nh,hd,L=qt.shape
    full=lambda *s: pl.BlockSpec(s,lambda i:(0,0,0))
    return pl.pallas_call(functools.partial(bwd_kernel,BQ,BK),grid=(L//BQ,),
      in_specs=[full(nh,hd,L),full(nh,L,hd),full(nh,hd,L),full(nh,L,hd),full(nh,L,hd),full(nh,hd,L),full(nh,L,hd),full(nh,1,L),full(nh,1,L)],
      out_specs=[pl.BlockSpec((nh,hd,BQ),lambda i:(0,0,i)),full(nh,L,hd),full(nh,L,hd)],
      out_shape=[jax.ShapeDtypeStruct((nh,hd,L),bf),jax.ShapeDtypeStruct((nh,L,hd),bf),jax.ShapeDtypeStruct((nh,L,hd),bf)],
      scratch_shapes=[pltpu.VMEM((nh,L,hd),f32)]*2,
      compiler_params=pltpu.CompilerParams(vmem_limit_bytes=62<<20),name=f"bwd{BQ}_{BK}")(qt,q,kt,k,v,dot_,do,lse,delta)


def body(
    inputs,
    w_query,
    w_key,
    w_value,
    w_proj,
    w_up,
    w_down,
    gain_first,
    gain_second,
    bias_up,
    bias_down,
    query_scale,
    cotangent,
):
    groups = lax.axis_size("seq")
    rows_of = lax.axis_size("fsdp")
    nh = H // groups
    cols = nh * HD
    both = ("seq", "fsdp")
    tokens, width = inputs.shape[1], inputs.shape[2]
    length = tokens * groups
    shard = w_query.shape[0]
    x_low = inputs.reshape(tokens, width)
    x_all = lax.all_gather(x_low, "seq", axis=0, tiled=True)
    qkv_rows = jnp.stack([w_query, w_key, w_value], 1).astype(bf).reshape(shard, 3, groups, cols)
    qkv_cols = lax.all_to_all(qkv_rows, "seq", split_axis=2, concat_axis=0, tiled=False)
    qkv_cols = lax.all_gather(qkv_cols, "fsdp", axis=1)
    qkv_w = qkv_cols.reshape(width, 3, cols).transpose(1, 0, 2)
    small = jnp.stack([gain_first, gain_second, bias_up, bias_down], 0).astype(bf)
    small = lax.all_gather(small, both, axis=1, tiled=True).astype(f32)
    first_gain, second_gain, upbias, downbias = small[0], small[1], small[2], small[3]
    proj_w = lax.all_gather(w_proj.astype(bf), both, axis=0, tiled=True)
    up_w = lax.all_gather(w_up.astype(bf), both, axis=0, tiled=True)
    down_w = lax.all_gather(w_down.astype(bf), both, axis=0, tiled=True)
    scale_dims = jax.nn.softplus(query_scale) * log_two_inverse / math.sqrt(HD)
    scale_cols = jnp.tile(scale_dims, nh)

    normed = rms_scale(x_all.astype(f32), first_gain).astype(bf)
    query_full = jnp.dot(normed, qkv_w[0], preferred_element_type=f32)
    query_low = (query_full * scale_cols).astype(bf)
    key_low = jnp.dot(normed, qkv_w[1], preferred_element_type=f32).astype(bf)
    value_low = jnp.dot(normed, qkv_w[2], preferred_element_type=f32).astype(bf)

    def by_head(a):
        return a.reshape(length, nh, HD).transpose(1, 0, 2)

    def flip(a):
        return jnp.swapaxes(a, 1, 2)

    q, k, v = by_head(query_low), by_head(key_low), by_head(value_low)
    qt, kt, vt = flip(q), flip(k), flip(v)
    ot, lse = flash_fwd(qt, k, vt, min(1024, length), min(512, length))
    mixed = lax.all_to_all(ot.reshape(cols, length), "seq", split_axis=1, concat_axis=0, tiled=True)
    float_in = x_low.astype(f32)
    middle = float_in + dot(mixed, proj_w, 0, 0)
    second = rms_scale(middle, second_gain).astype(bf)
    hidden = jnp.dot(second, up_w, preferred_element_type=f32) + upbias
    active = jax.nn.silu(hidden).astype(bf)
    result = middle + jnp.dot(active, down_w, preferred_element_type=f32) + downbias

    top_low = cotangent.reshape(tokens, width)
    grad_top = top_low.astype(f32)
    grad_bdown = jnp.sum(grad_top, axis=0)
    grad_wdown = dot(active, top_low, 0, 0)
    grad_active = dot(top_low, down_w, 1, 1)
    gate = 1 / (1 + jnp.exp(-hidden))
    grad_hidden = grad_active * (gate * (1 + hidden * (1 - gate)))
    grad_bup = jnp.sum(grad_hidden, axis=0)
    hidden_low = grad_hidden.astype(bf)
    grad_wup = dot(second, hidden_low, 0, 0)
    grad_second_in = dot(hidden_low, up_w, 1, 1)
    unused_second, second_pull = jax.vjp(rms_scale, middle, second_gain)
    grad_middle, grad_gsecond = second_pull(grad_second_in)
    grad_middle = grad_middle + grad_top
    middle_low = grad_middle.astype(bf)
    grad_wproj = dot(mixed, middle_low, 1, 0)
    grad_mixed = dot(proj_w, middle_low, 1, 1).astype(bf)
    dmt = lax.all_to_all(grad_mixed, "seq", split_axis=0, concat_axis=1, tiled=True)
    dmt = dmt.reshape(nh, HD, length)
    owned = [
        lax.psum_scatter(g.astype(bf), both, scatter_dimension=0, tiled=True).astype(f32)
        for g in (grad_wproj, grad_wup, grad_wdown)
    ]
    delta = jnp.sum(dmt.astype(f32) * ot.astype(f32), axis=1, keepdims=True)
    dqt, dk, dv = flash_bwd(
        qt, q, kt, k, v, dmt, flip(dmt), lse, delta, min(512, length), min(512, length)
    )

    def flat(a):
        return a.transpose(1, 0, 2).reshape(length, cols)

    dqs = flat(flip(dqt)).astype(f32)
    dq = (dqs * scale_cols).astype(bf)
    dk, dv = flat(dk), flat(dv)
    scale_part = jnp.sum(jnp.sum(dqs * query_full, axis=0).reshape(nh, HD), axis=0)
    grad_qkv = jnp.concatenate([dot(normed, g, 0, 0) for g in (dq, dk, dv)], 1)
    back = dot(dq, qkv_w[0], 1, 1) + dot(dk, qkv_w[1], 1, 1) + dot(dv, qkv_w[2], 1, 1)
    back = lax.psum_scatter(back.astype(bf), "seq", scatter_dimension=0, tiled=True).astype(f32)
    grad_qkv = grad_qkv.reshape(groups, rows_of, shard, 3 * cols)
    grad_qkv = lax.psum_scatter(grad_qkv, "fsdp", scatter_dimension=1, tiled=False)
    grad_qkv = lax.all_to_all(grad_qkv, "seq", split_axis=0, concat_axis=0, tiled=False)
    grad_qkv = grad_qkv.reshape(groups, shard, 3, cols).transpose(2, 1, 0, 3).reshape(3, shard, width)
    unused_first, first_pull = jax.vjp(rms_scale, float_in, first_gain)
    grad_below, grad_gfirst = first_pull(back)
    grad_inputs = (grad_middle + grad_below).astype(bf)
    scale_row = jnp.pad(scale_part, (0, width - HD))
    vectors = jnp.stack([grad_gfirst, grad_gsecond, grad_bup, grad_bdown, scale_row], 0)
    vectors = lax.psum(vectors, both)
    at = (lax.axis_index("seq") * rows_of + lax.axis_index("fsdp")) * shard
    mine = lax.dynamic_slice_in_dim(vectors, at, shard, 1)
    grad_scale = vectors[4, :HD] * jax.nn.sigmoid(query_scale) * log_two_inverse / math.sqrt(HD)
    return (
        result.astype(bf).reshape(inputs.shape),
        grad_inputs.reshape(inputs.shape),
        grad_qkv[0],
        grad_qkv[1],
        grad_qkv[2],
        owned[0],
        owned[1],
        owned[2],
        mine[0],
        mine[1],
        mine[2],
        mine[3],
        grad_scale,
    )


def solution(mesh):
    return jax.shard_map(
        body,
        mesh=mesh,
        in_specs=(
            P("fsdp", "seq", None),
            P(("seq", "fsdp"), None),
            P(("seq", "fsdp"), None),
            P(("seq", "fsdp"), None),
            P(("seq", "fsdp"), None),
            P(("seq", "fsdp"), None),
            P(("seq", "fsdp"), None),
            P(("seq", "fsdp")),
            P(("seq", "fsdp")),
            P(("seq", "fsdp")),
            P(("seq", "fsdp")),
            P(),
            P("fsdp", "seq", None),
        ),
        out_specs=(
            P("fsdp", "seq", None),
            P("fsdp", "seq", None),
            P(("seq", "fsdp"), None),
            P(("seq", "fsdp"), None),
            P(("seq", "fsdp"), None),
            P(("seq", "fsdp"), None),
            P(("seq", "fsdp"), None),
            P(("seq", "fsdp"), None),
            P(("seq", "fsdp")),
            P(("seq", "fsdp")),
            P(("seq", "fsdp")),
            P(("seq", "fsdp")),
            P(),
        ),
        check_vma=False,
    )
```

time: 1590 us -> 1130 us (0.71)
  matrix products: 496 us -> 113 us
  waiting for transfers between devices: 366 us -> 681 us
  other arithmetic: 316 us -> 35.3 us
  local copies, waits for them, and re-layouts: 211 us -> 52.2 us
  Pallas kernels: 0 us -> 94.6 us
  blocking collectives: 154 us -> 121 us
    dot_general x74 -> x18, matrix products: 496 us -> 113 us  [the longest x13 80.5 us: dot(): lax.dot_general(a, b, (((ca,), (cb,)), ((), ())), preferred_element_type=...]
    reduce_scatter x6 -> x4, waiting for transfers between devices: 238 us -> 489 us  [the longest x3 407 us: body(): lax.psum_scatter(g.astype(bf), both, scatter_dimension=0, tiled=True)]
    unnamed x10 -> x3, other arithmetic: 133 us -> 0.01 us
    convert_element_type x26 -> x10, other arithmetic: 118 us -> 14.3 us  [the longest x1 6.93 us: body(): normed = rms_scale(x_all.astype(f32), first_gain).astype(bf)]
    pallas_call x0 -> x2, Pallas kernels: none -> 94.6 us  [the longest x1 60.5 us: flash_bwd(): pl.pallas_call(functools.partial(bwd_kernel, BQ, BK), grid=(L // BQ,), in...]
    unnamed x2 -> x0, blocking collectives: 83.1 us -> none
    unnamed x115 -> x90, local copies, waits for them, and re-layouts: 86.7 us -> 9.4 us
    all_gather x0 -> x1, blocking collectives: none -> 67 us  [body(): small = lax.all_gather(small, both, axis=1, tiled=True).astype(f32)]
  transfers between devices with their start and end apart: 17 -> 13, of which waited for: 8 -> 11; matrix products, arithmetic and copies ran while one was open for 62% -> 12% of each run, Pallas kernels for 0% -> 3%
where the time goes in v1:
time: 1130 us; the launch traced here: 1120 us
  waiting for transfers between devices  681 us (60%)
  blocking collectives  121 us (11%)
  matrix products  113 us (10%)
  Pallas kernels  94.6 us (8%)
  local copies, waits for them, and re-layouts  52.2 us (5%)
  other arithmetic  35.3 us (3%)
  between operations  15.2 us (1%)
  starting transfers between devices  12.5 us (1%)
    reduce_scatter x3, waiting for transfers between devices, body(): lax.psum_scatter(g.astype(bf), both, scatter_dimension=0, tiled=True)  407 us
    reduce_scatter x1, waiting for transfers between devices, body(): lax.psum_scatter(back.astype(bf), 'seq', scatter_dimension=0, tiled=True)  82.8 us
    dot_general x13, matrix products, dot(): lax.dot_general(a, b, (((ca,), (cb,)), ((), ())), preferred_element_type=...  80.5 us
    all_gather x1, blocking collectives, body(): small = lax.all_gather(small, both, axis=1, tiled=True).astype(f32)  67 us
    pallas_call x1, Pallas kernels, flash_bwd(): pl.pallas_call(functools.partial(bwd_kernel, BQ, BK), grid=(L // BQ,), in...  60.5 us
    all_gather x1, waiting for transfers between devices, body(): down_w = lax.all_gather(w_down.astype(bf), both, axis=0, tiled=True)  55.2 us
    unnamed x11, waiting for transfers between devices  41.7 us
    psum x1, blocking collectives, body(): vectors = lax.psum(vectors, both)  39.7 us
  transfers between devices with their start and end apart: 13, of which 11 were waited for; matrix products, arithmetic and copies ran while one was open for 12% of the time, Pallas kernels for 3%

profile of v1, /device:TPU:0, one launch (start us, length us, event | category | flops | bytes accessed | tf_op | source)
XLA Modules:
  0.0 1124.9 jit_solution(12686710737189071668)
XLA Ops:
  11.1 14.5 %all_to_all.55 = bf16[1,40,3,8,160]{4,1,2,0,3:T(8,128)(2,1)} all-to-all(bf16[1,40,3,8,160]{4,1,2,0,3:T(8,128)(2,1)S(1)} %copy.168), channel_id=1, replica_groups=mesh['seq'=8,'fsdp'=4] {'seq'}, dimensions={3} | all-to-all | bytes 614400 | tf_op jit(solution)/shard_map/all_to_all | solution.py:137
  28.7 67.0 %all-gather.2 = bf16[32,40,4]{1,2,0:T(4,128)(2,1)S(1)} all-gather(bf16[1,40,4]{1,2,0:T(4,128)(2,1)S(1)} %maximum_bitcast_fusion), channel_id=1, replica_groups=mesh['seq'=8,'fsdp'=4] {'seq','fsdp'}, dimensions={0}, use_global_device_ids=true | all-gather | bytes 10560 | tf_op jit(solution)/shard_map/all_gather | solution.py:141
  98.3 34.8 %all-gather.15.cloned.1.call-done = bf16[1,4096,1280]{2,1,0:T(8,128)(2,1)} async-done(((bf16[1,512,1280]{2,1,0:T(8,128)(2,1)}), bf16[1,4096,1280]{2,1,0:T(8,128)(2,1)}) %all-gather.15.cloned.1.call-update) | async-done | bytes 10485776 | tf_op jit(solution)/shard_map/all_gather | solution.py:135
  139.2 6.9 fusion.2
  152.5 9.0 convolution_convert_fusion.3
  161.6 6.7 multiply_convert_fusion.4
  168.3 34.1 %fwd1024_512.1 = (bf16[2,80,4096]{2,1,0:T(8,128)(2,1)}, f32[2,1,4096]{2,1,0:T(1,128)}) custom-call(bf16[2,80,4096]{2,1,0:T(8,128)(2,1)} %bitcast.154, bf16[2,4096,80]{2,1,0:T(8,128)(2,1)} %bitcast.159, bf16[2,80,4096]{2,1,0:T(8,128)(2,1)} %bitcast.171), custom_call_target="tpu_custom_call" | custom-call | tf_op jit(solution)/shard_map/fwd1024_512/pallas_call | solution.py:63
  209.3 19.6 %all-to-all-done.1 = bf16[160,8,512]{2,0,1:T(8,128)(2,1)S(1)} async-done(((bf16[160,8,512]{2,0,1:T(8,128)(2,1)}), bf16[160,8,512]{2,0,1:T(8,128)(2,1)S(1)}, u32[]{:S(2)}, u32[]{:S(2)}) %all-to-all-start.1) | async-done | bytes 1310752 | tf_op jit(solution)/shard_map/all_to_all | solution.py:164
  234.8 23.6 %all-gather.11.cloned.1.call-done = bf16[1280,1280]{1,0:T(8,128)(2,1)} async-done(((bf16[40,1280]{1,0:T(8,128)(2,1)}), bf16[1280,1280]{1,0:T(8,128)(2,1)}) %all-gather.11.cloned.1.call-update) | async-done | bytes 3276816 | tf_op jit(solution)/shard_map/all_gather | solution.py:144
  258.5 6.3 convolution_add_fusion.1
  264.7 55.2 %all-gather.13.cloned.1.call-done = bf16[1280,1280]{1,0:T(8,128)(2,1)} async-done(((bf16[40,1280]{1,0:T(8,128)(2,1)}), bf16[1280,1280]{1,0:T(8,128)(2,1)}) %all-gather.13.cloned.1.call-update) | async-done | bytes 3276816 | tf_op jit(solution)/shard_map/all_gather | solution.py:145
  344.2 11.6 %all-to-all-done.2 = bf16[8,160,512]{2,1,0:T(8,128)(2,1)} async-done(((bf16[8,160,512]{2,1,0:T(8,128)(2,1)}), bf16[8,160,512]{2,1,0:T(8,128)(2,1)}, u32[]{:S(2)}, u32[]{:S(2)}) %all-to-all-start.2) | async-done | bytes 1310752 | tf_op jit(solution)/shard_map/all_to_all | solution.py:189
  366.6 60.5 %bwd512_512.1 = (bf16[2,80,4096]{2,1,0:T(8,128)(2,1)}, bf16[2,4096,80]{2,1,0:T(8,128)(2,1)}, bf16[2,4096,80]{2,1,0:T(8,128)(2,1)}) custom-call(bf16[2,80,4096]{2,1,0:T(8,128)(2,1)} %bitcast.155, bf16[2,4096,80]{2,1,0:T(8,128)(2,1)} %bitcast.177, bf16[2,80,4096]{2,1,0:T(8,128)(2,1)} %bitcast.170, bf16[2,4096,80]{2,1,0:T(8,128)(2,1)} %bitcast.160, ...), custom_call_target="tpu_custom_call" | custom-call | tf_op jit(solution)/shard_map/bwd512_512/pallas_call | solution.py:103
  435.1 6.4 fusion.33
  471.6 11.4 %fusion.25 = f32[4096,1280]{1,0:T(8,128)} fusion(bf16[4096,160]{0,1:T(8,128)(2,1)} %bitcast.167, bf16[3,1280,160]{2,1,0:T(8,128)(2,1)S(1)} %bitcast.164), kind=kOutput, calls=%fused_computation.64 | convolution fusion | flops 1677721600 | bytes 22937600 | tf_op jit(solution)/shard_map/dot_general | solution.py:25
  483.4 8.7 fusion.23
  492.1 19.0 %add_convert_fusion = bf16[4096,1280]{1,0:T(8,128)(2,1)} fusion(f32[4096,1280]{1,0:T(8,128)} %fusion.23, f32[4096,1280]{1,0:T(8,128)} %fusion.25, bf16[4096,160]{0,1:T(8,128)(2,1)S(1)} %bitcast.158, bf16[3,1280,160]{2,1,0:T(8,128)(2,1)S(1)} %bitcast.166), kind=kOutput, calls=%fused_computation.5 | convolution fusion | flops 1693450240 | bytes 54394880 | tf_op jit(solution)/shard_map/dot_general | solution.py:25
  512.7 40.9 %all-reduce.4.cloned.1.call-done = f32[8,4,40,480]{3,2,1,0:T(8,128)} async-done(((f32[8,4,40,480]{3,2,1,0:T(8,128)}), f32[8,4,40,480]{3,2,1,0:T(8,128)}) %all-reduce.4.cloned.1.call-update) | async-done | bytes 2457616
  560.2 6.9 fusion.7
  576.7 121.3 %reduce-scatter.10.cloned.1.call-done = bf16[40,1280]{1,0:T(8,128)(2,1)} async-done(((bf16[1280,1280]{1,0:T(8,128)(2,1)}), bf16[40,1280]{1,0:T(8,128)(2,1)}) %reduce-scatter.10.cloned.1.call-update) | async-done | bytes 102416 | tf_op jit(solution)/shard_map/reduce_scatter | solution.py:192
  699.6 142.8 %reduce-scatter.12.cloned.1.call-done = bf16[40,1280]{1,0:T(8,128)(2,1)} async-done(((bf16[1280,1280]{1,0:T(8,128)(2,1)}), bf16[40,1280]{1,0:T(8,128)(2,1)}) %reduce-scatter.12.cloned.1.call-update) | async-done | bytes 102416 | tf_op jit(solution)/shard_map/reduce_scatter | solution.py:192
  844.0 142.5 %reduce-scatter.8.cloned.1.call-done = bf16[40,1280]{1,0:T(8,128)(2,1)} async-done(((bf16[1280,1280]{1,0:T(8,128)(2,1)}), bf16[40,1280]{1,0:T(8,128)(2,1)}) %reduce-scatter.8.cloned.1.call-update) | async-done | bytes 102416 | tf_op jit(solution)/shard_map/reduce_scatter | solution.py:192
  988.0 82.8 %reduce-scatter.6.cloned.1.call-done = bf16[512,1280]{1,0:T(8,128)(2,1)} async-done(((bf16[4096,1280]{1,0:T(8,128)(2,1)}), bf16[512,1280]{1,0:T(8,128)(2,1)}) %reduce-scatter.6.cloned.1.call-update) | async-done | bytes 1310736 | tf_op jit(solution)/shard_map/reduce_scatter | solution.py:209
  1073.4 39.7 %psum.7 = f32[5,1280]{1,0:T(8,128)S(1)} all-reduce(f32[5,1280]{1,0:T(8,128)S(1)} %stack.58), channel_id=1, replica_groups=mesh['seq'=8,'fsdp'=4] {'seq','fsdp'}, use_global_device_ids=true, to_apply=%region_17.18 | all-reduce | flops 6400 | bytes 51200 | tf_op jit(solution)/shard_map/psum | solution.py:219
  (200 shorter events, 137.4 us)
Async XLA Ops:
  7.2 89.3 %all-gather.17.cloned.1.call-start = ((), (), s32[]{:S(2)}) async-start(), calls=%async_computation.16 | async-start | bytes 2457600 | tf_op jit(solution)/shard_map/all_gather | solution.py:138
  10.9 17.7 %copy-start.28 = (f32[40]{0:T(128)S(1)}, f32[40]{0:T(128)}, u32[]{:S(2)}) copy-start(f32[40]{0:T(128)} %param.21) | copy-start | bytes 484
  10.9 17.7 %copy-start.29 = (f32[40]{0:T(128)S(1)}, f32[40]{0:T(128)}, u32[]{:S(2)}) copy-start(f32[40]{0:T(128)} %param.20) | copy-start | bytes 484
  11.0 17.7 %copy-start.30 = (f32[40]{0:T(128)S(1)}, f32[40]{0:T(128)}, u32[]{:S(2)}) copy-start(f32[40]{0:T(128)} %param.23) | copy-start | bytes 484
  25.6 107.5 %all-gather.15.cloned.1.call-start = ((), (), s32[]{:S(2)}) async-start(), calls=%async_computation.15 | async-start | bytes 11796480 | tf_op jit(solution)/shard_map/all_gather | solution.py:135
  26.3 183.0 %all-gather.9.cloned.1.call-start = ((), (), s32[]{:S(2)}) async-start(), calls=%async_computation.8 | async-start | bytes 3379200 | tf_op jit(solution)/shard_map/all_gather | solution.py:143
  27.1 231.4 %all-gather.11.cloned.1.call-start = ((), (), s32[]{:S(2)}) async-start(), calls=%async_computation.9 | async-start | bytes 3379200 | tf_op jit(solution)/shard_map/all_gather | solution.py:144
  27.8 292.2 %all-gather.13.cloned.1.call-start = ((), (), s32[]{:S(2)}) async-start(), calls=%async_computation.10 | async-start | bytes 3379200 | tf_op jit(solution)/shard_map/all_gather | solution.py:145
  96.5 42.7 %copy-start.25 = (f32[1280]{0:T(1024)}, f32[1280]{0:T(1024)S(1)}, u32[]{:S(2)}) copy-start(f32[1280]{0:T(1024)S(1)} %get-tuple-element.30) | copy-start | bytes 15364
  98.3 47.9 %copy-start.7 = (bf16[8,4,40,3,1,160]{5,2,1,0,3,4:T(8,128)(2,1)}, bf16[8,4,40,3,1,160]{5,2,1,0,3,4:T(8,128)(2,1)S(1)}, u32[]{:S(2)}) copy-start(bf16[8,4,40,3,1,160]{5,2,1,0,3,4:T(8,128)(2,1)S(1)} %copy.170) | copy-start | bytes 3686404
  204.2 24.7 %copy-start.3 = (bf16[1,512,1280]{2,1,0:T(8,128)(2,1)S(1)}, bf16[1,512,1280]{2,1,0:T(8,128)(2,1)}, u32[]{:S(2)}) copy-start(bf16[1,512,1280]{2,1,0:T(8,128)(2,1)} %param.13) | copy-start | bytes 3932164
  205.7 23.2 %all-to-all-start.1 = ((bf16[160,8,512]{2,0,1:T(8,128)(2,1)}), bf16[160,8,512]{2,0,1:T(8,128)(2,1)S(1)}, u32[]{:S(2)}, u32[]{:S(2)}) async-start(bf16[160,8,512]{2,0,1:T(8,128)(2,1)} %copy.175), calls=%async_computation.1 | async-start | bytes 2621440 | tf_op jit(solution)/shard_map/all_to_all | solution.py:164
  258.4 61.5 %copy-start.20 = (bf16[1,512,1280]{2,1,0:T(8,128)(2,1)S(1)}, bf16[1,512,1280]{2,1,0:T(8,128)(2,1)}, u32[]{:S(2)}) copy-start(bf16[1,512,1280]{2,1,0:T(8,128)(2,1)} %param.25) | copy-start | bytes 3932164
  333.1 22.7 %all-to-all-start.2 = ((bf16[8,160,512]{2,1,0:T(8,128)(2,1)}), bf16[8,160,512]{2,1,0:T(8,128)(2,1)}, u32[]{:S(2)}, u32[]{:S(2)}) async-start(bf16[8,160,512]{2,1,0:T(8,128)(2,1)} %bitcast.181), calls=%async_computation.2 | async-start | bytes 2621440 | tf_op jit(solution)/shard_map/all_to_all | solution.py:189
  337.5 216.0 %all-reduce.4.cloned.1.call-start = ((), (), s32[]{:S(2)}) async-start(), calls=%async_computation.17 | async-start | bytes 5242880
  451.3 246.7 %reduce-scatter.10.cloned.1.call-start = ((), (), s32[]{:S(2)}) async-start(), calls=%async_computation.13 | async-start | bytes 3379200 | tf_op jit(solution)/shard_map/reduce_scatter | solution.py:192
  456.9 385.5 %reduce-scatter.12.cloned.1.call-start = ((), (), s32[]{:S(2)}) async-start(), calls=%async_computation.14 | async-start | bytes 3379200 | tf_op jit(solution)/shard_map/reduce_scatter | solution.py:192
  463.5 522.9 %reduce-scatter.8.cloned.1.call-start = ((), (), s32[]{:S(2)}) async-start(), calls=%async_computation.12 | async-start | bytes 3379200 | tf_op jit(solution)/shard_map/reduce_scatter | solution.py:192
  470.1 600.7 %reduce-scatter.6.cloned.1.call-start = ((), (), s32[]{:S(2)}) async-start(), calls=%async_computation.11 | async-start | bytes 11796480 | tf_op jit(solution)/shard_map/reduce_scatter | solution.py:209
  511.2 49.0 %copy-start.27 = (f32[1280]{0:T(1024)S(1)}, f32[1280]{0:T(1024)}, u32[]{:S(2)}) copy-start(f32[1280]{0:T(1024)} %get-tuple-element.28) | copy-start | bytes 15364
  556.2 16.2 %all-to-all-start.3 = ((f32[8,40,480]{2,1,0:T(8,128)}), f32[8,40,480]{2,1,0:T(8,128)S(1)}, u32[]{:S(2)}, u32[]{:S(2)}) async-start(f32[8,40,480]{2,1,0:T(8,128)} %dynamic-slice_bitcast_fusion), calls=%async_computation.4 | async-start | bytes 1310720 | tf_op jit(solution)/shard_map/all_to_all | solution.py:212
  573.8 497.0 %copy-start.26 = (f32[1280]{0:T(1024)S(1)}, f32[1280]{0:T(1024)}, u32[]{:S(2)}) copy-start(f32[1280]{0:T(1024)} %copy-done.25) | copy-start | bytes 15364
  574.9 538.2 %copy-start.34 = (f32[80]{0:T(128)S(1)}, f32[80]{0:T(128)}, u32[]{:S(2)}) copy-start(f32[80]{0:T(128)} %param.24) | copy-start | bytes 964
  1070.8 43.4 %copy-start.17 = (bf16[512,1280]{1,0:T(8,128)(2,1)S(1)}, bf16[512,1280]{1,0:T(8,128)(2,1)}, u32[]{:S(2)}) copy-start(bf16[512,1280]{1,0:T(8,128)(2,1)} %reduce-scatter.6.cloned.1.call-done) | copy-start | bytes 3932164
  (33 other events, 243.2 us)
Sparse Core Ops, SparseCore 0:
  25.7 43.2 all-gather.16
  70.9 62.1 all-gather.14
  136.5 59.3 all-gather.8
  199.1 59.2 all-gather.10
  261.7 58.2 all-gather.12
  451.4 102.1 all-reduce.3
  555.9 142.0 reduce-scatter.9
  700.4 141.9 reduce-scatter.11
  844.7 141.7 reduce-scatter.7
  990.2 80.5 reduce-scatter.5

commit v2 on v1

--- a/solution.py
+++ b/solution.py
@@ -106,6 +106,404 @@
       out_shape=[jax.ShapeDtypeStruct((nh,hd,L),bf),jax.ShapeDtypeStruct((nh,L,hd),bf),jax.ShapeDtypeStruct((nh,L,hd),bf)],
       scratch_shapes=[pltpu.VMEM((nh,L,hd),f32)]*2,
       compiler_params=pltpu.CompilerParams(vmem_limit_bytes=62<<20),name=f"bwd{BQ}_{BK}")(qt,q,kt,k,v,dot_,do,lse,delta)
+MESH = pl.DeviceIdType.MESH
+
+
+def spots():
+    s, f = lax.axis_index("seq"), lax.axis_index("fsdp")
+    return s, f, s // 2, lax.rem(s, 2)
+
+
+def greet(S, F):
+    s, f, _, _ = spots()
+    barrier = pltpu.get_barrier_semaphore()
+    for i in range(1, S):
+        pl.semaphore_signal(barrier, inc=1, device_id=(lax.rem(s + i, S), f), device_id_type=MESH)
+    for i in range(1, F):
+        pl.semaphore_signal(barrier, inc=1, device_id=(s, lax.rem(f + i, F)), device_id_type=MESH)
+    pl.semaphore_wait(barrier, S + F - 2)
+
+
+def remote(src, dst, sends, recvs, n, to):
+    return pltpu.make_async_remote_copy(
+        src_ref=src,
+        dst_ref=dst,
+        send_sem=sends.at[n],
+        recv_sem=recvs.at[n],
+        device_id=to,
+        device_id_type=MESH,
+    )
+
+
+def gather_kernel(S, F, x, wq, sm, wm, x_all, wq_all, sm_all, wm_all, xv, qv, sv, mv, local,
+                  xs, xr, qs, qr, ss, sr, ms, mr):
+    s, f, p, c = spots()
+    P_ = S // 2
+    other = 1 - c
+    loads = [
+        pltpu.make_async_copy(sm, sv, local.at[0]),
+        pltpu.make_async_copy(wq, qv, local.at[1]),
+        pltpu.make_async_copy(x, xv, local.at[2]),
+        pltpu.make_async_copy(wm, mv, local.at[3]),
+    ]
+    for load in loads:
+        load.start()
+    greet(S, F)
+    mate = (p * 2 + other, f)
+    todo = []
+
+    def go(copy):
+        copy.start()
+        todo.append(copy)
+
+    def chip(i):
+        return lax.rem(p + i, P_) * 2 + c
+
+    def back(i):
+        return lax.rem(p + P_ - i, P_) * 2 + c
+
+    def deep(i):
+        return lax.rem(f + i, F)
+
+    def behind(i):
+        return lax.rem(f + F - i, F)
+
+    loads[0].wait()
+    keep0 = pltpu.make_async_copy(sv, sm_all.at[s, f], local.at[0])
+    keep0.start()
+    for i in range(1, F):
+        go(remote(sv, sm_all.at[s, f], ss, sr, i, (s, deep(i))))
+    loads[1].wait()
+    keep1 = pltpu.make_async_copy(qv.at[s], wq_all.at[s, f], local.at[1])
+    keep1.start()
+    for i in range(1, S):
+        to = lax.rem(s + i, S)
+        go(remote(qv.at[to], wq_all.at[s, f], qs, qr, i, (to, f)))
+    loads[2].wait()
+    keep2 = pltpu.make_async_copy(xv, x_all.at[s], local.at[2])
+    keep2.start()
+    for i in range(1, P_):
+        go(remote(xv, x_all.at[s], xs, xr, i, (chip(i), f)))
+    go(remote(xv, x_all.at[s], xs, xr, 0, mate))
+    loads[3].wait()
+    keep3 = pltpu.make_async_copy(mv, wm_all.at[:, s, f], local.at[3])
+    keep3.start()
+    for i in range(1, F):
+        go(remote(mv, wm_all.at[:, s, f], ms, mr, i, (s, deep(i))))
+    for i in range(1, F):
+        g = behind(i)
+        remote(sv, sm_all.at[s, g], ss, sr, i, mate).wait_recv()
+    keep0.wait()
+    for i in range(1, S):
+        go(remote(sm_all.at[s], sm_all.at[s], ss, sr, F - 1 + i, (lax.rem(s + i, S), f)))
+    for i in range(1, S):
+        remote(qv.at[0], wq_all.at[lax.rem(s + S - i, S), f], qs, qr, i, mate).wait_recv()
+    keep1.wait()
+    for i in range(1, F):
+        go(remote(wq_all.at[:, f], wq_all.at[:, f], qs, qr, S - 1 + i, (s, deep(i))))
+    for i in range(1, F):
+        remote(mv, wm_all.at[:, s, behind(i)], ms, mr, i, mate).wait_recv()
+    keep3.wait()
+    for i in range(1, P_):
+        go(remote(wm_all.at[:, s], wm_all.at[:, s], ms, mr, F - 1 + i, (chip(i), f)))
+    go(remote(wm_all.at[:, s], wm_all.at[:, s], ms, mr, 0, mate))
+    for i in range(1, P_):
+        src = back(i)
+        remote(xv, x_all.at[src], xs, xr, i, mate).wait_recv()
+        go(remote(x_all.at[src], x_all.at[src], xs, xr, P_ - 1 + i, mate))
+    for i in range(1, P_):
+        src = back(i)
+        remote(wm_all.at[:, s], wm_all.at[:, src], ms, mr, F - 1 + i, mate).wait_recv()
+        go(remote(wm_all.at[:, src], wm_all.at[:, src], ms, mr, F + P_ - 2 + i, mate))
+    for i in range(1, S):
+        src = lax.rem(s + S - i, S)
+        remote(sm_all.at[src], sm_all.at[src], ss, sr, F - 1 + i, mate).wait_recv()
+    for i in range(1, F):
+        g = behind(i)
+        remote(wq_all.at[:, g], wq_all.at[:, g], qs, qr, S - 1 + i, mate).wait_recv()
+    near = p * 2 + other
+    remote(xv, x_all.at[near], xs, xr, 0, mate).wait_recv()
+    remote(wm_all.at[:, s], wm_all.at[:, near], ms, mr, 0, mate).wait_recv()
+    for i in range(1, P_):
+        src = lax.rem(p + P_ - i, P_) * 2 + other
+        remote(xv, x_all.at[src], xs, xr, P_ - 1 + i, mate).wait_recv()
+        remote(wm_all.at[:, s], wm_all.at[:, src], ms, mr, F + P_ - 2 + i, mate).wait_recv()
+    keep2.wait()
+    for copy in todo:
+        copy.wait_send()
+
+
+def gather_all(S, F, x, wq, sm, wm):
+    any_ = pl.BlockSpec(memory_space=pl.ANY)
+    shapes = [
+        (S,) + x.shape,
+        (S, F) + wq.shape[1:],
+        (S, F) + sm.shape,
+        (wm.shape[0], S, F) + wm.shape[1:],
+    ]
+    P_ = S // 2
+    dma = pltpu.SemaphoreType.DMA
+    counts = [2 * P_ - 1, S + F - 1, F + S - 1, F + 2 * P_ - 2]
+    sems = []
+    for n in counts:
+        sems += [dma((n + 1,)), dma((n + 1,))]
+    return pl.pallas_call(
+        functools.partial(gather_kernel, S, F),
+        out_shape=[
+            jax.ShapeDtypeStruct(sh, a.dtype) for sh, a in zip(shapes, (x, wq, sm, wm), strict=True)
+        ],
+        in_specs=[any_] * 4,
+        out_specs=[any_] * 4,
+        scratch_shapes=[
+            pltpu.VMEM(x.shape, x.dtype),
+            pltpu.VMEM(wq.shape, wq.dtype),
+            pltpu.VMEM(sm.shape, sm.dtype),
+            pltpu.VMEM(wm.shape, wm.dtype),
+            dma((4,)),
+        ]
+        + sems,
+        compiler_params=pltpu.CompilerParams(collective_id=1, has_side_effects=True),
+        name="gather",
+    )(x, wq, sm, wm)
+
+
+def scatter_kernel(S, F, g, b, q, vec, g_out, b_out, q_out, vec_out,
+                   gm, gi, bm, bi, gp, bp, gz, qm, qi, qt_, qo, vi, vz, vp, vo, go_, bo, local,
+                   gs, gr, bs, br, qs, qr, vs, vr):
+    s, f, p, c = spots()
+    P_ = S // 2
+    other = 1 - c
+    mate = (p * 2 + other, f)
+    todo = []
+
+    def go(copy):
+        copy.start()
+        todo.append(copy)
+
+    def chip(i):
+        return lax.rem(p + i, P_)
+
+    def deep(i):
+        return lax.rem(f + i, F)
+
+    def behind(i):
+        return lax.rem(f + F - i, F)
+
+    lq = pltpu.make_async_copy(q, qm, local.at[0])
+    lq.start()
+    lv = pltpu.make_async_copy(vec, vi, local.at[1])
+    lv.start()
+    order = list(range(1, P_)) + [0]
+    own = []
+    for n, i in enumerate(order):
+        t = chip(i)
+        own.append(
+            (
+                pltpu.make_async_copy(g.at[:, t * 2 + c], gm.at[i], local.at[2 + 2 * n]),
+                pltpu.make_async_copy(b.at[t * 2 + c], bm.at[i], local.at[3 + 2 * n]),
+            )
+        )
+        own[-1][0].start()
+        own[-1][1].start()
+    greet(S, F)
+    lv.wait()
+    for i in range(1, F):
+        go(remote(vi, vz.at[i], vs, vr, i, (s, deep(i))))
+    for n, i in enumerate(order):
+        t = chip(i)
+        go(remote(g.at[:, t * 2 + other], gi.at[i], gs, gr, i, mate))
+        go(remote(b.at[t * 2 + other], bi.at[i], bs, br, i, mate))
+    lq.wait()
+    for i in range(1, F):
+        go(remote(qm.at[:, deep(i)], qi.at[i], qs, qr, i, (s, deep(i))))
+
+    def add_slabs(n, at_dst, at_parts, kind):
+        def one(k, _):
+            total = at_parts[0](k)
+            for part in at_parts[1:]:
+                total = total + part(k)
+            at_dst(k, total.astype(kind))
+            return 0
+
+        lax.fori_loop(0, n, one, 0)
+
+    NW, R = g.shape[0], g.shape[3]
+    T = b.shape[1]
+    step = 64 if T % 64 == 0 else T
+
+    def flat_g(k):
+        return lax.div(k, F), lax.rem(k, F)
+
+    for n, i in enumerate(order):
+        t = chip(i)
+        own[n][0].wait()
+        remote(g.at[:, s], gi.at[i], gs, gr, i, mate).wait_recv()
+
+        def put(k, v, i=i):
+            w, z = flat_g(k)
+            gm[i, w, z] = v
+
+        def left(k, i=i):
+            w, z = flat_g(k)
+            return gm[i, w, z].astype(f32)
+
+        def right(k, i=i):
+            w, z = flat_g(k)
+            return gi[i, w, z].astype(f32)
+
+        add_slabs(NW * F, put, [left, right], bf)
+        if i:
+            go(remote(gm.at[i], gp.at[i], gs, gr, P_ + i, (t * 2 + c, f)))
+        own[n][1].wait()
+        remote(b.at[s], bi.at[i], bs, br, i, mate).wait_recv()
+
+        def putb(k, v, i=i):
+            bm[i, pl.ds(k * step, step), :] = v
+
+        def leftb(k, i=i):
+            return bm[i, pl.ds(k * step, step), :].astype(f32)
+
+        def rightb(k, i=i):
+            return bi[i, pl.ds(k * step, step), :].astype(f32)
+
+        add_slabs(T // step, putb, [leftb, rightb], bf)
+        if i:
+            go(remote(bm.at[i], bp.at[i], bs, br, P_ + i, (t * 2 + c, f)))
+    total = vi[...]
+    for i in range(1, F):
+        remote(vi, vz.at[i], vs, vr, i, mate).wait_recv()
+    for i in range(1, F):
+        total = total + vz[i]
+    vp[0] = total
+    for i in range(1, S):
+        go(remote(vp.at[0], vp.at[i], vs, vr, F - 1 + i, (lax.rem(s + i, S), f)))
+    for i in range(1, F):
+        remote(qm.at[:, f], qi.at[i], qs, qr, i, mate).wait_recv()
+
+    def put_q(k, v):
+        qt_[k] = v
+
+    add_slabs(
+        S,
+        put_q,
+        [lambda k: qm[k, f].astype(f32)]
+        + [lambda k, i=i: qi[i, k].astype(f32) for i in range(1, F)],
+        bf,
+    )
+    keep = pltpu.make_async_copy(qt_.at[s], qo.at[s], local.at[0])
+    keep.start()
+    for i in range(1, S):
+        to = lax.rem(s + i, S)
+        go(remote(qt_.at[to], qo.at[s], qs, qr, F - 1 + i, (to, f)))
+    for i in range(1, P_):
+        remote(gm.at[0], gp.at[i], gs, gr, P_ + i, mate).wait_recv()
+
+    def put_g(k, v):
+        w, z = flat_g(k)
+        gp[0, w, z] = v
+
+    def part_g(i):
+        def read(k):
+            w, z = flat_g(k)
+            return (gm if i == 0 else gp)[i, w, z].astype(f32)
+
+        return read
+
+    add_slabs(NW * F, put_g, [part_g(i) for i in range(P_)], bf)
+    for i in range(1, F):
+        go(remote(gp.at[0, :, deep(i)], gz.at[i], gs, gr, 2 * P_ + i, (s, deep(i))))
+    for i in range(1, P_):
+        remote(bm.at[0], bp.at[i], bs, br, P_ + i, mate).wait_recv()
+
+    def put_b(k, v):
+        bo[pl.ds(k * step, step), :] = v
+
+    def part_b(i):
+        def read(k):
+            return (bm if i == 0 else bp)[i, pl.ds(k * step, step), :].astype(f32)
+
+        return read
+
+    add_slabs(T // step, put_b, [part_b(i) for i in range(P_)], f32)
+    outs = [pltpu.make_async_copy(bo, b_out, local.at[1])]
+    outs[0].start()
+    total = vp[0]
+    for i in range(1, S):
+        remote(vp.at[0], vp.at[i], vs, vr, F - 1 + i, mate).wait_recv()
+    for i in range(1, S):
+        total = total + vp[i]
+    vo[...] = total
+    outs.append(pltpu.make_async_copy(vo, vec_out, local.at[2]))
+    outs[1].start()
+    for i in range(1, S):
+        src = lax.rem(s + S - i, S)
+        remote(qt_.at[0], qo.at[src], qs, qr, F - 1 + i, mate).wait_recv()
+    keep.wait()
+    outs.append(pltpu.make_async_copy(qo, q_out, local.at[3]))
+    outs[2].start()
+    for i in range(1, F):
+        remote(gp.at[0, :, f], gz.at[i], gs, gr, 2 * P_ + i, mate).wait_recv()
+    for w in range(NW):
+        total = gp[0, w, f].astype(f32)
+        for i in range(1, F):
+            total = total + gz[i, w].astype(f32)
+        go_[w] = total
+    outs.append(pltpu.make_async_copy(go_, g_out, local.at[4]))
+    outs[3].start()
+    for out in outs:
+        out.wait()
+    for copy in todo:
+        copy.wait_send()
+
+
+def scatter_all(S, F, g, b, q, vec):
+    any_ = pl.BlockSpec(memory_space=pl.ANY)
+    P_ = S // 2
+    NW, R, D = g.shape[0], g.shape[3], g.shape[4]
+    T = b.shape[1]
+    C3 = q.shape[3]
+    dma = pltpu.SemaphoreType.DMA
+    counts = [2 * P_ + F, 2 * P_, F + S, F + S]
+    sems = []
+    for n in counts:
+        sems += [dma((n,)), dma((n,))]
+    V = pltpu.VMEM
+    return pl.pallas_call(
+        functools.partial(scatter_kernel, S, F),
+        out_shape=[
+            jax.ShapeDtypeStruct((NW, R, D), f32),
+            jax.ShapeDtypeStruct((T, D), f32),
+            jax.ShapeDtypeStruct((S, R, C3), bf),
+            jax.ShapeDtypeStruct(vec.shape, f32),
+        ],
+        in_specs=[any_] * 4,
+        out_specs=[any_] * 4,
+        scratch_shapes=[
+            V((P_, NW, F, R, D), bf),
+            V((P_, NW, F, R, D), bf),
+            V((P_, T, D), bf),
+            V((P_, T, D), bf),
+            V((P_, NW, F, R, D), bf),
+            V((P_, T, D), bf),
+            V((F, NW, R, D), bf),
+            V((S, F, R, C3), bf),
+            V((F, S, R, C3), bf),
+            V((S, R, C3), bf),
+            V((S, R, C3), bf),
+            V(vec.shape, f32),
+            V((F,) + vec.shape, f32),
+            V((S,) + vec.shape, f32),
+            V(vec.shape, f32),
+            V((NW, R, D), f32),
+            V((T, D), f32),
+            dma((2 + 2 * P_ + 4,)),
+        ]
+        + sems,
+        compiler_params=pltpu.CompilerParams(
+            collective_id=2, has_side_effects=True, vmem_limit_bytes=60 << 20
+        ),
+        name="scatter",
+    )(g, b, q, vec)
 
 
 def body(
@@ -132,21 +530,24 @@
     length = tokens * groups
     shard = w_query.shape[0]
     x_low = inputs.reshape(tokens, width)
-    x_all = lax.all_gather(x_low, "seq", axis=0, tiled=True)
     qkv_rows = jnp.stack([w_query, w_key, w_value], 1).astype(bf).reshape(shard, 3, groups, cols)
-    qkv_cols = lax.all_to_all(qkv_rows, "seq", split_axis=2, concat_axis=0, tiled=False)
-    qkv_cols = lax.all_gather(qkv_cols, "fsdp", axis=1)
-    qkv_w = qkv_cols.reshape(width, 3, cols).transpose(1, 0, 2)
-    small = jnp.stack([gain_first, gain_second, bias_up, bias_down], 0).astype(bf)
-    small = lax.all_gather(small, both, axis=1, tiled=True).astype(f32)
+    qkv_rows = qkv_rows.transpose(2, 0, 1, 3).reshape(groups, shard, 3 * cols)
+    small = jnp.stack([gain_first, gain_second, bias_up, bias_down], 0)
+    small = jnp.pad(small, ((0, 4), (0, 128 - shard)))
+    weights = jnp.stack([w_proj, w_up, w_down], 0).astype(bf)
+    x_all, qkv_w, small, weights = gather_all(groups, rows_of, x_low, qkv_rows, small, weights)
+    x_all = x_all.reshape(length, width)
+    qkv_w = qkv_w.reshape(width, 3, cols).transpose(1, 0, 2)
+    small = small[:, :, :4, :shard].transpose(2, 0, 1, 3).reshape(4, width).astype(bf).astype(f32)
     first_gain, second_gain, upbias, downbias = small[0], small[1], small[2], small[3]
-    proj_w = lax.all_gather(w_proj.astype(bf), both, axis=0, tiled=True)
-    up_w = lax.all_gather(w_up.astype(bf), both, axis=0, tiled=True)
-    down_w = lax.all_gather(w_down.astype(bf), both, axis=0, tiled=True)
+    weights = weights.reshape(3, width, width)
+    proj_w, up_w, down_w = weights[0], weights[1], weights[2]
     scale_dims = jax.nn.softplus(query_scale) * log_two_inverse / math.sqrt(HD)
     scale_cols = jnp.tile(scale_dims, nh)
 
-    normed = rms_scale(x_all.astype(f32), first_gain).astype(bf)
+    x_wide = x_all.astype(f32)
+    hat = x_wide * lax.rsqrt(jnp.mean(x_wide * x_wide, axis=-1, keepdims=True) + eps_norm)
+    normed = (hat * first_gain).astype(bf)
     query_full = jnp.dot(normed, qkv_w[0], preferred_element_type=f32)
     query_low = (query_full * scale_cols).astype(bf)
     key_low = jnp.dot(normed, qkv_w[1], preferred_element_type=f32).astype(bf)
@@ -188,10 +589,6 @@
     grad_mixed = dot(proj_w, middle_low, 1, 1).astype(bf)
     dmt = lax.all_to_all(grad_mixed, "seq", split_axis=0, concat_axis=1, tiled=True)
     dmt = dmt.reshape(nh, HD, length)
-    owned = [
-        lax.psum_scatter(g.astype(bf), both, scatter_dimension=0, tiled=True).astype(f32)
-        for g in (grad_wproj, grad_wup, grad_wdown)
-    ]
     delta = jnp.sum(dmt.astype(f32) * ot.astype(f32), axis=1, keepdims=True)
     dqt, dk, dv = flash_bwd(
         qt, q, kt, k, v, dmt, flip(dmt), lse, delta, min(512, length), min(512, length)
@@ -206,17 +603,24 @@
     scale_part = jnp.sum(jnp.sum(dqs * query_full, axis=0).reshape(nh, HD), axis=0)
     grad_qkv = jnp.concatenate([dot(normed, g, 0, 0) for g in (dq, dk, dv)], 1)
     back = dot(dq, qkv_w[0], 1, 1) + dot(dk, qkv_w[1], 1, 1) + dot(dv, qkv_w[2], 1, 1)
-    back = lax.psum_scatter(back.astype(bf), "seq", scatter_dimension=0, tiled=True).astype(f32)
-    grad_qkv = grad_qkv.reshape(groups, rows_of, shard, 3 * cols)
-    grad_qkv = lax.psum_scatter(grad_qkv, "fsdp", scatter_dimension=1, tiled=False)
-    grad_qkv = lax.all_to_all(grad_qkv, "seq", split_axis=0, concat_axis=0, tiled=False)
-    grad_qkv = grad_qkv.reshape(groups, shard, 3, cols).transpose(2, 1, 0, 3).reshape(3, shard, width)
+    scale_row = jnp.pad(scale_part, (0, width - HD))
+    zeros = jnp.zeros_like(scale_row)
+    grad_gfirst = jnp.sum(back * hat, axis=0)
+    vectors = jnp.stack([grad_gfirst, grad_gsecond, grad_bup, grad_bdown, scale_row, zeros, zeros, zeros], 0)
+    stacked = jnp.stack([grad_wproj.astype(bf), grad_wup.astype(bf), grad_wdown.astype(bf)], 0)
+    owned, back, grad_qkv, vectors = scatter_all(
+        groups,
+        rows_of,
+        stacked.reshape(3, groups, rows_of, shard, width),
+        back.astype(bf).reshape(groups, tokens, width),
+        grad_qkv.astype(bf).reshape(groups, rows_of, shard, 3 * cols),
+        vectors,
+    )
+    grad_qkv = grad_qkv.reshape(groups, shard, 3, cols).transpose(2, 1, 0, 3)
+    grad_qkv = grad_qkv.reshape(3, shard, width).astype(f32)
     unused_first, first_pull = jax.vjp(rms_scale, float_in, first_gain)
-    grad_below, grad_gfirst = first_pull(back)
+    grad_below, unused_gain = first_pull(back)
     grad_inputs = (grad_middle + grad_below).astype(bf)
-    scale_row = jnp.pad(scale_part, (0, width - HD))
-    vectors = jnp.stack([grad_gfirst, grad_gsecond, grad_bup, grad_bdown, scale_row], 0)
-    vectors = lax.psum(vectors, both)
     at = (lax.axis_index("seq") * rows_of + lax.axis_index("fsdp")) * shard
     mine = lax.dynamic_slice_in_dim(vectors, at, shard, 1)
     grad_scale = vectors[4, :HD] * jax.nn.sigmoid(query_scale) * log_two_inverse / math.sqrt(HD)

time: 1130 us -> 598 us (0.53)
  waiting for transfers between devices: 681 us -> 8.8 us
  Pallas kernels: 94.6 us -> 345 us
  blocking collectives: 121 us -> 0 us
  local copies, waits for them, and re-layouts: 52.2 us -> 74.5 us
  between operations: 15.2 us -> 1.83 us
  other arithmetic: 35.3 us -> 47.9 us
    reduce_scatter x4 -> x0, waiting for transfers between devices: 489 us -> none  [the longest x3 407 us: body(): lax.psum_scatter(g.astype(bf), both, scatter_dimension=0, tiled=True)]
    pallas_call x0 -> x2, Pallas kernels: none -> 251 us  [the longest x1 126 us: gather_all(): pl.pallas_call(functools.partial(gather_kernel, S, F), out_shape=[jax.Sha...]
    all_gather x5 -> x0, waiting for transfers between devices: 114 us -> none  [the longest x1 55.2 us: body(): down_w = lax.all_gather(w_down.astype(bf), both, axis=0, tiled=True)]
    all_gather x1 -> x0, blocking collectives: 67 us -> none  [body(): small = lax.all_gather(small, both, axis=1, tiled=True).astype(f32)]
    unnamed x11 -> x0, waiting for transfers between devices: 41.7 us -> none
    psum x1 -> x0, blocking collectives: 39.7 us -> none  [body(): vectors = lax.psum(vectors, both)]
    all_to_all x1, waiting for transfers between devices: 19.6 us -> 0.01 us  [body(): lax.all_to_all(ot.reshape(cols, length), 'seq', split_axis=1, concat_axis...]
    slice x0 -> x5, local copies, waits for them, and re-layouts: none -> 17.8 us  [the longest x2 6.7 us: body(): value_low = jnp.dot(normed, qkv_w[2], preferred_element_type=f32).astype(bf)]
  transfers between devices with their start and end apart: 13 -> 2, of which waited for: 11 -> 1; matrix products, arithmetic and copies ran while one was open for 12% -> 6% of each run, Pallas kernels for 3% -> 0%
where the time goes in v2:
time: 598 us; the launch traced here: 589 us
  Pallas kernels  345 us (58%)
  matrix products  102 us (17%)
  local copies, waits for them, and re-layouts  74.5 us (12%)
  other arithmetic  47.9 us (8%)
  waiting for transfers between devices  8.8 us (1%)
  starting transfers between devices  8.51 us (1%)
    pallas_call x1, Pallas kernels, gather_all(): pl.pallas_call(functools.partial(gather_kernel, S, F), out_shape=[jax.Sha...  126 us
    pallas_call x1, Pallas kernels, scatter_all(): pl.pallas_call(functools.partial(scatter_kernel, S, F), out_shape=[jax.Sh...  124 us
    dot_general x13, matrix products, dot(): lax.dot_general(a, b, (((ca,), (cb,)), ((), ())), preferred_element_type=...  79.6 us
    pallas_call x1, Pallas kernels, flash_bwd(): pl.pallas_call(functools.partial(bwd_kernel, BQ, BK), grid=(L // BQ,), in...  60.6 us
    pallas_call x1, Pallas kernels, flash_fwd(): pl.pallas_call(functools.partial(fwd_kernel, BQ, BK), grid=(L // BQ,), in...  34.2 us
    dot_general x1, local copies, waits for them, and re-layouts, dot(): lax.dot_general(a, b, (((ca,), (cb,)), ((), ())), preferred_element_type=...  14.3 us
  transfers between devices with their start and end apart: 2, of which 1 were waited for; matrix products, arithmetic and copies ran while one was open for 6% of the time, Pallas kernels for 0%

profile of v2, /device:TPU:0, one launch (start us, length us, event | category | flops | bytes accessed | tf_op | source)
XLA Modules:
  0.0 589.3 jit_solution(18248252189197008515)
XLA Ops:
  10.5 126.3 %gather.1 = (bf16[8,512,1280]{2,1,0:T(8,128)(2,1)}, bf16[8,4,40,480]{3,2,1,0:T(8,128)(2,1)}, f32[8,4,8,128]{3,2,1,0:T(8,128)}, bf16[3,8,4,40,1280]{4,3,2,1,0:T(8,128)(2,1)}) custom-call(bf16[512,1280]{1,0:T(8,128)(2,1)} %bitcast.180, bf16[8,40,480]{2,1,0:T(8,128)(2,1)} %reshape.271.wq, f32[8,128]{1,0:T(8,128)} %select_maximum_fusion.sm, ...), custom_call_target="tpu_custom_call" | custom-call | tf_op jit(solution)/shard_map/gather/pallas_call | solution.py:250
  138.0 6.1 %multiply_reduce_fusion = f32[8,512]{1,0:T(8,128)S(1)} fusion(bf16[8,512,1280]{2,1,0:T(8,128)(2,1)} %get-tuple-element.26), kind=kLoop, calls=%fused_computation.5 | loop fusion | flops 15724544 | bytes 10502144 | tf_op jit(solution)/shard_map/reduce_sum | solution.py:549
  144.1 5.8 reshape.272
  161.2 6.7 %multiply_convert_fusion = bf16[8,512,1280]{2,1,0:T(8,128)(2,1)S(1)} fusion(f32[1280]{0:T(1024)S(1)} %mul.193, f32[8,512]{1,0:T(8,128)S(1)} %get-tuple-element.64, bf16[8,512,1280]{2,1,0:T(8,128)(2,1)} %get-tuple-element.26), kind=kLoop, calls=%fused_computation.4 | loop fusion | flops 20971520 | bytes 20993024 | tf_op jit(solution)/shard_map/convert_element_type | solution.py:550
  167.9 4.6 convolution_convert_fusion.3
  178.6 9.4 %multiply_convert_fusion.4 = (bf16[4096,160]{0,1:T(8,128)(2,1)}, f32[4096,160]{0,1:T(8,128)}) fusion(f32[160]{0:T(256)S(1)} %mul.196, bf16[4096,1280]{1,0:T(8,128)(2,1)} %bitcast.172, bf16[1,1280,160]{1,2,0:T(8,128)(2,1)S(1)} %copy.93), kind=kOutput, calls=%fused_computation.41 | convolution fusion | flops 1679032320 | bytes 14828160 | tf_op jit(solution)/shard_map/dot_general | solution.py:551
  188.0 34.2 %fwd1024_512.1 = (bf16[2,80,4096]{2,1,0:T(8,128)(2,1)}, f32[2,1,4096]{2,1,0:T(1,128)}) custom-call(bf16[2,80,4096]{2,1,0:T(8,128)(2,1)} %bitcast.177, bf16[2,4096,80]{2,1,0:T(8,128)(2,1)} %bitcast.181, bf16[2,80,4096]{2,1,0:T(8,128)(2,1)} %bitcast.201), custom_call_target="tpu_custom_call" | custom-call | tf_op jit(solution)/shard_map/fwd1024_512/pallas_call | solution.py:63
  225.5 4.4 all-to-all-start
  235.1 14.3 %copy.104 = bf16[1280,4096]{1,0:T(8,128)(2,1)} copy(bf16[1280,4096]{0,1:T(8,128)(2,1)} %bitcast.173) | data formatting | bytes 20971520 | tf_op jit(solution)/shard_map/dot_general | solution.py:25
  249.4 6.5 %fusion.32 = (bf16[1,8,4,40,1280]{4,3,2,1,0:T(8,128)(2,1)}, bf16[1,8,4,40,1280]{4,3,2,1,0:T(8,128)(2,1)}, bf16[1,8,4,40,1280]{4,3,2,1,0:T(8,128)(2,1)S(1)}) fusion(bf16[3,8,4,40,1280]{4,3,2,1,0:T(8,128)(2,1)} %get-tuple-element.30), kind=kLoop, calls=%fused_computation.99 | loop fusion | bytes 19660800 | tf_op jit(solution)/shard_map/slice | solution.py:544
  278.1 4.9 convolution_convert_fusion.2
  286.3 4.1 all-to-all-start.1
  290.4 9.4 %pad_maximum_fusion.g = bf16[3,8,4,40,1280]{4,3,2,1,0:T(8,128)(2,1)} fusion(bf16[1,8,4,40,1280]{4,3,2,1,0:T(8,128)(2,1)} %bitcast.210, bf16[1,8,4,40,1280]{4,3,2,1,0:T(8,128)(2,1)} %bitcast.209, bf16[1,8,4,40,1280]{4,3,2,1,0:T(8,128)(2,1)} %bitcast.213), kind=kLoop, calls=%fused_computation.6 | loop fusion | flops 9830400 | bytes 19660800 | tf_op jit(solution)/shard_map/stack | solution.py:610
  299.8 8.8 %all-to-all-done.1 = bf16[8,160,512]{2,1,0:T(8,128)(2,1)S(1)} async-done(((bf16[8,160,512]{2,1,0:T(8,128)(2,1)}), bf16[8,160,512]{2,1,0:T(8,128)(2,1)S(1)}, u32[]{:S(2)}, u32[]{:S(2)}) %all-to-all-start.1) | async-done | bytes 1310752 | tf_op jit(solution)/shard_map/all_to_all | solution.py:590
  316.4 60.6 %bwd512_512.1 = (bf16[2,80,4096]{2,1,0:T(8,128)(2,1)}, bf16[2,4096,80]{2,1,0:T(8,128)(2,1)}, bf16[2,4096,80]{2,1,0:T(8,128)(2,1)}) custom-call(bf16[2,80,4096]{2,1,0:T(8,128)(2,1)} %bitcast.178, bf16[2,4096,80]{2,1,0:T(8,128)(2,1)} %bitcast.193, bf16[2,80,4096]{2,1,0:T(8,128)(2,1)} %bitcast.200, bf16[2,4096,80]{2,1,0:T(8,128)(2,1)} %bitcast.182, ...), custom_call_target="tpu_custom_call" | custom-call | tf_op jit(solution)/shard_map/bwd512_512/pallas_call | solution.py:103
  381.5 4.0 copy.102
  385.5 4.0 copy.103
  391.8 7.4 %convolution_convert_fusion.6 = bf16[8,4,40,160]{3,2,1,0:T(8,128)(2,1)S(1)} fusion(bf16[8,4,40,4096]{3,2,1,0:T(8,128)(2,1)} %bitcast.184, bf16[4096,160,1,1]{0,1,3,2:T(8,128)(2,1)} %bitcast.190), kind=kOutput, calls=%fused_computation.42 | convolution fusion | flops 1677926400 | bytes 12206080 | tf_op jit(solution)/shard_map/dot_general | solution.py:25
  399.2 7.2 %convolution_convert_fusion.7 = bf16[8,4,40,160]{3,2,1,0:T(8,128)(2,1)S(1)} fusion(bf16[8,4,40,4096]{3,2,1,0:T(8,128)(2,1)} %bitcast.185, bf16[4096,160,1,1]{0,1,3,2:T(8,128)(2,1)S(1)} %bitcast.195), kind=kOutput, calls=%fused_computation.43 | convolution fusion | flops 1677926400 | bytes 12206080 | tf_op jit(solution)/shard_map/dot_general | solution.py:25
  409.7 8.6 %fusion.23 = f32[4096,1280]{1,0:T(8,128)} fusion(bf16[4096,160]{0,1:T(8,128)(2,1)S(1)} %bitcast.198, bf16[1,1280,160]{1,2,0:T(8,128)(2,1)S(1)} %copy-done.15), kind=kOutput, calls=%fused_computation.60 | convolution fusion | flops 1677721600 | bytes 22691840 | tf_op jit(solution)/shard_map/dot_general | solution.py:25
  418.4 10.5 %fusion.20 = f32[4096,1280]{1,0:T(8,128)} fusion(bf16[4096,160]{0,1:T(8,128)(2,1)S(1)} %bitcast.196, bf16[1,1280,160]{1,2,0:T(8,128)(2,1)S(1)} %copy-done.19), kind=kOutput, calls=%fused_computation.57 | convolution fusion | flops 1677721600 | bytes 22691840 | tf_op jit(solution)/shard_map/dot_general | solution.py:25
  428.9 18.7 %fusion.1 = (f32[1280]{0:T(1024)S(1)}, bf16[4096,1280]{1,0:T(8,128)(2,1)}) fusion(f32[4096]{0:T(1024)S(1)} %bitcast.216, bf16[8,512,1280]{2,1,0:T(8,128)(2,1)S(1)} %bitcast.169, bf16[4096,160]{0,1:T(8,128)(2,1)S(1)} %bitcast.191, bf16[1,1280,160]{1,2,0:T(8,128)(2,1)S(1)} %copy-done.21, f32[4096,1280]{1,0:T(8,128)} %fusion.23, f32[4096,1280]{1,0:T(8,128)} %fusion.20), kind=kOutput, calls=%fused_computation.2 | convolution fusion | flops 1714420480 | bytes 64656384 | tf_op jit(solution)/shard_map/dot_general | solution.py:25
  450.1 124.3 %scatter.1 = (f32[3,40,1280]{2,1,0:T(8,128)}, f32[512,1280]{1,0:T(8,128)}, bf16[8,40,480]{2,1,0:T(8,128)(2,1)}, f32[8,1280]{1,0:T(8,128)}) custom-call(bf16[3,8,4,40,1280]{4,3,2,1,0:T(8,128)(2,1)} %pad_maximum_fusion.g, bf16[8,512,1280]{2,1,0:T(8,128)(2,1)} %bitcast.174, bf16[8,4,40,480]{3,2,1,0:T(8,128)(2,1)} %pad_maximum_fusion.1.q, f32[8,1280]{1,0:T(8,128)} %stack.96.vec), custom_call_target="tpu_custom_call" | custom-call | tf_op jit(solution)/shard_map/scatter/pallas_call | solution.py:471
  584.6 4.3 fusion.10
  (165 shorter events, 92.5 us)
Async XLA Ops:
  138.0 23.2 %copy-start.27 = (f32[1280]{0:T(1024)}, f32[1280]{0:T(1024)S(1)}, u32[]{:S(2)}) copy-start(f32[1280]{0:T(1024)S(1)} %mul.193) | copy-start | bytes 15364
  156.6 11.3 %copy-start.20 = (bf16[1,1280,160]{1,2,0:T(8,128)(2,1)}, bf16[1,1280,160]{1,2,0:T(8,128)(2,1)S(1)}, u32[]{:S(2)}) copy-start(bf16[1,1280,160]{1,2,0:T(8,128)(2,1)S(1)} %copy.96) | copy-start | bytes 1228804
  159.4 13.2 %copy-start.18 = (bf16[1,1280,160]{1,2,0:T(8,128)(2,1)}, bf16[1,1280,160]{1,2,0:T(8,128)(2,1)S(1)}, u32[]{:S(2)}) copy-start(bf16[1,1280,160]{1,2,0:T(8,128)(2,1)S(1)} %copy.94) | copy-start | bytes 1228804
  161.2 17.4 %copy-start.14 = (bf16[1,1280,160]{1,2,0:T(8,128)(2,1)}, bf16[1,1280,160]{1,2,0:T(8,128)(2,1)S(1)}, u32[]{:S(2)}) copy-start(bf16[1,1280,160]{1,2,0:T(8,128)(2,1)S(1)} %copy.93) | copy-start | bytes 1228804
  176.1 11.9 %copy-start.9 = (bf16[4096,160]{0,1:T(8,128)(2,1)}, bf16[4096,160]{0,1:T(8,128)(2,1)S(1)}, u32[]{:S(2)}) copy-start(bf16[4096,160]{0,1:T(8,128)(2,1)S(1)} %convolution_convert_fusion.4) | copy-start | bytes 3932164
  224.0 6.2 %copy-start.10 = (bf16[4096,160]{0,1:T(8,128)(2,1)S(1)}, bf16[4096,160]{0,1:T(8,128)(2,1)}, u32[]{:S(2)}) copy-start(bf16[4096,160]{0,1:T(8,128)(2,1)} %convolution_convert_fusion.3) | copy-start | bytes 3932164
  225.5 7.2 %copy-start.1 = (bf16[4096,160]{0,1:T(8,128)(2,1)S(1)}, bf16[4096,160]{0,1:T(8,128)(2,1)}, u32[]{:S(2)}) copy-start(bf16[4096,160]{0,1:T(8,128)(2,1)} %get-tuple-element.71) | copy-start | bytes 3932164
  225.5 30.4 %all-to-all-start = ((bf16[160,8,512]{2,0,1:T(8,128)(2,1)}), bf16[160,8,512]{2,0,1:T(8,128)(2,1)}, u32[]{:S(2)}, u32[]{:S(2)}) async-start(bf16[160,8,512]{2,0,1:T(8,128)(2,1)} %copy.97), calls=%async_computation | async-start | bytes 2621440 | tf_op jit(solution)/shard_map/all_to_all | solution.py:565
  286.3 22.3 %all-to-all-start.1 = ((bf16[8,160,512]{2,1,0:T(8,128)(2,1)}), bf16[8,160,512]{2,1,0:T(8,128)(2,1)S(1)}, u32[]{:S(2)}, u32[]{:S(2)}) async-start(bf16[8,160,512]{2,1,0:T(8,128)(2,1)} %bitcast.37), calls=%async_computation.1 | async-start | bytes 2621440 | tf_op jit(solution)/shard_map/all_to_all | solution.py:590
  381.5 8.0 %copy-start.4 = (f32[4096,160]{0,1:T(8,128)S(1)}, f32[4096,160]{0,1:T(8,128)}, u32[]{:S(2)}) copy-start(f32[4096,160]{0,1:T(8,128)} %get-tuple-element.72) | copy-start | bytes 7864324
  391.7 7.5 %copy-start.7 = (bf16[4096,2,80]{0,2,1:T(8,128)(2,1)S(1)}, bf16[4096,2,80]{0,2,1:T(8,128)(2,1)}, u32[]{:S(2)}) copy-start(bf16[4096,2,80]{0,2,1:T(8,128)(2,1)} %copy.102) | copy-start | bytes 3932164
  391.7 14.7 %slice-start.3 = ((s8[10485760]{0:T(1024)(128)(4,1)}), s8[4194304]{0:T(1024)(128)(4,1)S(1)}, s32[]{:S(2)}) async-start(s8[10485760]{0:T(1024)(128)(4,1)} %bitcast.186), calls=%async_computation.5 | async-start | bytes 8388608
  391.7 14.7 %slice-start.4 = ((s8[10485760]{0:T(1024)(128)(4,1)}), s8[4194304]{0:T(1024)(128)(4,1)S(1)}, s32[]{:S(2)}) async-start(s8[10485760]{0:T(1024)(128)(4,1)} %bitcast.186), calls=%async_computation.6 | async-start | bytes 8388608
  399.2 7.3 %slice-start.5 = ((s8[10485760]{0:T(1024)(128)(4,1)}), s8[2097152]{0:T(1024)(128)(4,1)S(1)}, s32[]{:S(2)}) async-start(s8[10485760]{0:T(1024)(128)(4,1)} %bitcast.186), calls=%async_computation.7 | async-start | bytes 4194304
  399.2 7.3 %copy-start.8 = (bf16[2,80,4096]{2,1,0:T(8,128)(2,1)S(1)}, bf16[2,80,4096]{2,1,0:T(8,128)(2,1)}, u32[]{:S(2)}) copy-start(bf16[2,80,4096]{2,1,0:T(8,128)(2,1)} %multiply_convert_fusion.1) | copy-start | bytes 3932164
  409.7 8.6 %copy-start.19 = (bf16[1,1280,160]{1,2,0:T(8,128)(2,1)S(1)}, bf16[1,1280,160]{1,2,0:T(8,128)(2,1)}, u32[]{:S(2)}) copy-start(bf16[1,1280,160]{1,2,0:T(8,128)(2,1)} %copy-done.18) | copy-start | bytes 1228804
  418.4 10.5 %slice-start = ((s8[10485760]{0:T(1024)(128)(4,1)}), s8[4194304]{0:T(1024)(128)(4,1)S(1)}, s32[]{:S(2)}) async-start(s8[10485760]{0:T(1024)(128)(4,1)} %bitcast.168), calls=%async_computation.2 | async-start | bytes 8388608
  418.4 10.5 %slice-start.1 = ((s8[10485760]{0:T(1024)(128)(4,1)}), s8[4194304]{0:T(1024)(128)(4,1)S(1)}, s32[]{:S(2)}) async-start(s8[10485760]{0:T(1024)(128)(4,1)} %bitcast.168), calls=%async_computation.3 | async-start | bytes 8388608
  418.4 10.5 %slice-start.2 = ((s8[10485760]{0:T(1024)(128)(4,1)}), s8[2097152]{0:T(1024)(128)(4,1)S(1)}, s32[]{:S(2)}) async-start(s8[10485760]{0:T(1024)(128)(4,1)} %bitcast.168), calls=%async_computation.4 | async-start | bytes 4194304
  418.4 10.5 %copy-start.6 = (bf16[4096,2,80]{0,2,1:T(8,128)(2,1)S(1)}, bf16[4096,2,80]{0,2,1:T(8,128)(2,1)}, u32[]{:S(2)}) copy-start(bf16[4096,2,80]{0,2,1:T(8,128)(2,1)} %copy.103) | copy-start | bytes 3932164
  418.4 10.5 %copy-start.21 = (bf16[1,1280,160]{1,2,0:T(8,128)(2,1)S(1)}, bf16[1,1280,160]{1,2,0:T(8,128)(2,1)}, u32[]{:S(2)}) copy-start(bf16[1,1280,160]{1,2,0:T(8,128)(2,1)} %copy-done.20) | copy-start | bytes 1228804
  450.1 124.4 %copy-start.33 = (f32[80]{0:T(128)S(1)}, f32[80]{0:T(128)}, u32[]{:S(2)}) copy-start(f32[80]{0:T(128)} %param.24) | copy-start | bytes 964
  450.1 126.9 %copy-start.2 = (bf16[1,512,1280]{2,1,0:T(8,128)(2,1)S(1)}, bf16[1,512,1280]{2,1,0:T(8,128)(2,1)}, u32[]{:S(2)}) copy-start(bf16[1,512,1280]{2,1,0:T(8,128)(2,1)} %param.13) | copy-start | bytes 3932164
  450.1 126.9 %copy-start.28 = (f32[1280]{0:T(1024)S(1)}, f32[1280]{0:T(1024)}, u32[]{:S(2)}) copy-start(f32[1280]{0:T(1024)} %copy-done.27) | copy-start | bytes 15364
  (18 other events, 72.3 us)

commit v3 on v2

--- a/solution.py
+++ b/solution.py
@@ -23,48 +23,6 @@
 
 def dot(a,b,ca=1,cb=0):
     return lax.dot_general(a,b,(((ca,),(cb,)),((),())),preferred_element_type=f32)
-
-def fwd_kernel(BQ,BK,qt,k,vt,ot,lse):
-    nh,hd,L=qt.shape
-    i=pl.program_id(0)
-    q=[qt[h,:,pl.ds(pl.multiple_of(i*BQ,BQ),BQ)] for h in range(nh)]
-    def step(j,carry,diag=None):
-        out=[]
-        s=[]
-        for h in range(nh):
-            kk=k[h,pl.ds(pl.multiple_of(j*BK,BK),BK),:]
-            s.append(dot(kk,q[h]))
-        for h in range(nh):
-            m,l,acc=carry[h]
-            sh=s[h]
-            if diag is not None:
-                kp=lax.broadcasted_iota(jnp.int32,sh.shape,0)+diag*BK
-                qp=lax.broadcasted_iota(jnp.int32,sh.shape,1)
-                sh=jnp.where(kp<=qp,sh,NEG)
-            mn=jnp.maximum(m,jnp.max(sh,axis=0,keepdims=True))
-            a=jnp.exp(m-mn)
-            p=jnp.exp(sh-mn)
-            l=l*a+jnp.sum(p,axis=0,keepdims=True)
-            vv=vt[h,:,pl.ds(pl.multiple_of(j*BK,BK),BK)]
-            acc=acc*a+dot(vv,p.astype(bf))
-            out.append((mn,l,acc))
-        return tuple(out)
-    init=tuple((jnp.full((1,BQ),NEG,f32),jnp.zeros((1,BQ),f32),jnp.zeros((hd,BQ),f32)) for _ in range(nh))
-    r=BQ//BK
-    c=lax.fori_loop(0,i*r,step,init)
-    for d in range(r):
-        c=step(i*r+d,c,d)
-    for h in range(nh):
-        m,l,acc=c[h]
-        ot[h,:,:]=(acc/l).astype(bf)
-        lse[h,:,:]=m+jnp.log(l)
-def flash_fwd(qt,k,vt,BQ=512,BK=512):
-    nh,hd,L=qt.shape
-    return pl.pallas_call(functools.partial(fwd_kernel,BQ,BK),grid=(L//BQ,),
-      in_specs=[pl.BlockSpec((nh,hd,L),lambda i:(0,0,0)),pl.BlockSpec((nh,L,hd),lambda i:(0,0,0)),pl.BlockSpec((nh,hd,L),lambda i:(0,0,0))],
-      out_specs=[pl.BlockSpec((nh,hd,BQ),lambda i:(0,0,i)),pl.BlockSpec((nh,1,BQ),lambda i:(0,0,i))],
-      out_shape=[jax.ShapeDtypeStruct((nh,hd,L),bf),jax.ShapeDtypeStruct((nh,1,L),f32)],
-      compiler_params=pltpu.CompilerParams(vmem_limit_bytes=60<<20),name=f"fwd{BQ}_{BK}")(qt,k,vt)
 
 def bwd_kernel(BQ,BK,qt,q,kt,k,v,dot_,do,lse,delta,dqt,dk,dv,dks,dvs):
     nh,hd,L=qt.shape
@@ -186,10 +144,10 @@
         go(remote(xv, x_all.at[s], xs, xr, i, (chip(i), f)))
     go(remote(xv, x_all.at[s], xs, xr, 0, mate))
     loads[3].wait()
-    keep3 = pltpu.make_async_copy(mv, wm_all.at[:, s, f], local.at[3])
+    keep3 = pltpu.make_async_copy(mv, wm_all.at[:, f], local.at[3])
     keep3.start()
     for i in range(1, F):
-        go(remote(mv, wm_all.at[:, s, f], ms, mr, i, (s, deep(i))))
+        go(remote(mv, wm_all.at[:, f], ms, mr, i, (s, deep(i))))
     for i in range(1, F):
         g = behind(i)
         remote(sv, sm_all.at[s, g], ss, sr, i, mate).wait_recv()
@@ -202,19 +160,12 @@
     for i in range(1, F):
         go(remote(wq_all.at[:, f], wq_all.at[:, f], qs, qr, S - 1 + i, (s, deep(i))))
     for i in range(1, F):
-        remote(mv, wm_all.at[:, s, behind(i)], ms, mr, i, mate).wait_recv()
+        remote(mv, wm_all.at[:, behind(i)], ms, mr, i, mate).wait_recv()
     keep3.wait()
-    for i in range(1, P_):
-        go(remote(wm_all.at[:, s], wm_all.at[:, s], ms, mr, F - 1 + i, (chip(i), f)))
-    go(remote(wm_all.at[:, s], wm_all.at[:, s], ms, mr, 0, mate))
     for i in range(1, P_):
         src = back(i)
         remote(xv, x_all.at[src], xs, xr, i, mate).wait_recv()
         go(remote(x_all.at[src], x_all.at[src], xs, xr, P_ - 1 + i, mate))
-    for i in range(1, P_):
-        src = back(i)
-        remote(wm_all.at[:, s], wm_all.at[:, src], ms, mr, F - 1 + i, mate).wait_recv()
-        go(remote(wm_all.at[:, src], wm_all.at[:, src], ms, mr, F + P_ - 2 + i, mate))
     for i in range(1, S):
         src = lax.rem(s + S - i, S)
         remote(sm_all.at[src], sm_all.at[src], ss, sr, F - 1 + i, mate).wait_recv()
@@ -223,11 +174,9 @@
         remote(wq_all.at[:, g], wq_all.at[:, g], qs, qr, S - 1 + i, mate).wait_recv()
     near = p * 2 + other
     remote(xv, x_all.at[near], xs, xr, 0, mate).wait_recv()
-    remote(wm_all.at[:, s], wm_all.at[:, near], ms, mr, 0, mate).wait_recv()
     for i in range(1, P_):
         src = lax.rem(p + P_ - i, P_) * 2 + other
         remote(xv, x_all.at[src], xs, xr, P_ - 1 + i, mate).wait_recv()
-        remote(wm_all.at[:, s], wm_all.at[:, src], ms, mr, F + P_ - 2 + i, mate).wait_recv()
     keep2.wait()
     for copy in todo:
         copy.wait_send()
@@ -239,11 +188,11 @@
         (S,) + x.shape,
         (S, F) + wq.shape[1:],
         (S, F) + sm.shape,
-        (wm.shape[0], S, F) + wm.shape[1:],
+        (wm.shape[0], F) + wm.shape[1:],
     ]
     P_ = S // 2
     dma = pltpu.SemaphoreType.DMA
-    counts = [2 * P_ - 1, S + F - 1, F + S - 1, F + 2 * P_ - 2]
+    counts = [2 * P_ - 1, S + F - 1, F + S - 1, F]
     sems = []
     for n in counts:
         sems += [dma((n + 1,)), dma((n + 1,))]
@@ -506,6 +455,225 @@
     )(g, b, q, vec)
 
 
+def flip_bits(p, i):
+    out, bit = p, 1
+    while bit <= i:
+        if i & bit:
+            out = out + bit - 2 * bit * lax.rem(lax.div(p, bit), 2)
+        bit *= 2
+    return out
+
+
+def forward_kernel(S, F, nh, x_all, w, g1, sc, wz, n1, qt, kt, vt, ot, lse, mixed, wm,
+                   wt, kk, xb, nb, wv, inx, outn, local, osend, orecv, wsend, wrecv):
+    s, f, p, c = spots()
+    P_ = S // 2
+    T, D = x_all.shape[1], x_all.shape[2]
+    C = nh * HD
+    L = S * T
+    BQ = 2 * T
+    BK = min(512, BQ)
+    other = 1 - c
+    mate = (p * 2 + other, f)
+    load = pltpu.make_async_copy(wz, wv, local.at[0])
+    load.start()
+
+    def fetch(b):
+        return pltpu.make_async_copy(x_all.at[b], xb.at[lax.rem(b, 2)], inx.at[lax.rem(b, 2)])
+
+    def store(b):
+        return pltpu.make_async_copy(nb.at[lax.rem(b, 2)], n1.at[b], outn.at[lax.rem(b, 2)])
+
+    fetch(0).start()
+    greet(S, F)
+    load.wait()
+    keep = pltpu.make_async_copy(wv, wm.at[:, s], local.at[0])
+    keep.start()
+
+    def spread(i):
+        return remote(wv, wm.at[:, s], wsend, wrecv, i, (flip_bits(p, i) * 2 + c, f))
+
+    def forward(i):
+        src = flip_bits(p, i) * 2 + c
+        return remote(wm.at[:, src], wm.at[:, src], wsend, wrecv, P_ + i, mate)
+
+    for i in range(1, P_):
+        spread(P_ - i).start()
+    near = remote(wv, wm.at[:, s], wsend, wrecv, 0, mate)
+    near.start()
+    wt[...] = jnp.transpose(w[...])
+
+    rows = 64
+
+    def project(b, _):
+        slot = lax.rem(b, 2)
+        fetch(b).wait()
+
+        @pl.when(b + 1 < S)
+        def _():
+            fetch(b + 1).start()
+
+        @pl.when(b >= 2)
+        def _():
+            store(b - 2).wait()
+
+        def norm(k, _):
+            at = pl.ds(pl.multiple_of(k * rows, rows), rows)
+            v = xb[slot, at, :].astype(f32)
+            r = lax.rsqrt(jnp.mean(v * v, axis=-1, keepdims=True) + eps_norm)
+            nb[slot, at, :] = (v * r * g1[...]).astype(bf)
+            return 0
+
+        lax.fori_loop(0, T // rows, norm, 0)
+        store(b).start()
+        cols = pl.ds(pl.multiple_of(b * T, T), T)
+        res = dot(wt[...], nb[slot], 1, 1)
+        qt[:, cols] = (res[:C] * sc[...]).astype(bf)
+        kt[:, cols] = res[C : 2 * C].astype(bf)
+        vt[:, cols] = res[2 * C :].astype(bf)
+        for h in range(nh):
+            kk[h, cols, :] = jnp.transpose(res[C + h * HD : C + (h + 1) * HD]).astype(bf)
+        return 0
+
+    lax.fori_loop(0, S, project, 0)
+    store(S - 2).wait()
+    store(S - 1).wait()
+
+    def attend(t):
+        first = pl.multiple_of(t * BQ, BQ)
+        q = [qt[h * HD : (h + 1) * HD, pl.ds(first, BQ)] for h in range(nh)]
+
+        def step(j, carry, diag=None):
+            at = pl.ds(pl.multiple_of(j * BK, BK), BK)
+            scores = [dot(kk[h, at, :], q[h]) for h in range(nh)]
+            out = []
+            for h in range(nh):
+                m, l, acc = carry[h]
+                sh = scores[h]
+                if diag is not None:
+                    kp = lax.broadcasted_iota(jnp.int32, sh.shape, 0) + diag * BK
+                    qp = lax.broadcasted_iota(jnp.int32, sh.shape, 1)
+                    sh = jnp.where(kp <= qp, sh, NEG)
+                mn = jnp.maximum(m, jnp.max(sh, axis=0, keepdims=True))
+                a = jnp.exp(m - mn)
+                e = jnp.exp(sh - mn)
+                l = l * a + jnp.sum(e, axis=0, keepdims=True)
+                acc = acc * a + dot(vt[h * HD : (h + 1) * HD, at], e.astype(bf))
+                out.append((mn, l, acc))
+            return tuple(out)
+
+        carry = tuple(
+            (jnp.full((1, BQ), NEG, f32), jnp.zeros((1, BQ), f32), jnp.zeros((HD, BQ), f32))
+            for _ in range(nh)
+        )
+        r = BQ // BK
+        carry = lax.fori_loop(0, t * r, step, carry)
+        for d in range(r):
+            carry = step(t * r + d, carry, d)
+        for h in range(nh):
+            m, l, acc = carry[h]
+            ot[h * HD : (h + 1) * HD, pl.ds(first, BQ)] = (acc / l).astype(bf)
+            lse[h : h + 1, pl.ds(first, BQ)] = m + jnp.log(l)
+
+    def to_owner(src, n, to):
+        return pltpu.make_async_remote_copy(
+            src_ref=src,
+            dst_ref=mixed.at[s],
+            send_sem=osend.at[n],
+            recv_sem=orecv.at[n - n % 2 + c],
+            device_id=to,
+            device_id_type=MESH,
+        )
+
+    def send(i, half):
+        t = flip_bits(p, i)
+        src = ot.at[:, pl.ds(pl.multiple_of(t * BQ + half * T, T), T)]
+        return to_owner(src, 2 * i + half, (t * 2 + half, f))
+
+    for i in range(1, P_):
+        attend(flip_bits(p, P_ - i))
+        send(P_ - i, 0).start()
+        send(P_ - i, 1).start()
+        spread(P_ - i).wait_recv()
+        forward(P_ - i).start()
+    attend(p)
+    mine = ot.at[:, pl.ds(pl.multiple_of(s * T, T), T)]
+    theirs = ot.at[:, pl.ds(pl.multiple_of((p * 2 + other) * T, T), T)]
+    last = to_owner(theirs, 0, mate)
+    last.start()
+    own = pltpu.make_async_copy(mine, mixed.at[s], local.at[1])
+    own.start()
+    def from_source(i, core):
+        return pltpu.make_async_remote_copy(
+            src_ref=mine,
+            dst_ref=mixed.at[flip_bits(p, i) * 2 + core],
+            send_sem=osend.at[0],
+            recv_sem=orecv.at[2 * i + core],
+            device_id=mate,
+            device_id_type=MESH,
+        )
+
+    for i in range(1, P_):
+        for core in range(2):
+            from_source(i, core).wait_recv()
+    from_source(0, other).wait_recv()
+    last.wait_send()
+    own.wait()
+    keep.wait()
+    near.wait()
+    for i in range(1, P_):
+        forward(i).wait()
+        spread(i).wait_send()
+        send(i, 0).wait_send()
+        send(i, 1).wait_send()
+
+
+def forward_all(S, F, nh, x_all, w, g1, sc, wz):
+    T, D = x_all.shape[1], x_all.shape[2]
+    C = nh * HD
+    L = S * T
+    P_ = S // 2
+    any_ = pl.BlockSpec(memory_space=pl.ANY)
+    vm = pl.BlockSpec(memory_space=pltpu.VMEM)
+    dma = pltpu.SemaphoreType.DMA
+    shape = jax.ShapeDtypeStruct
+    NW, R = wz.shape[0], wz.shape[2]
+    V = pltpu.VMEM
+    return pl.pallas_call(
+        functools.partial(forward_kernel, S, F, nh),
+        out_shape=[
+            shape((S, T, D), bf),
+            shape((C, L), bf),
+            shape((C, L), bf),
+            shape((C, L), bf),
+            shape((C, L), bf),
+            shape((nh, L), f32),
+            shape((S, C, T), bf),
+            shape((NW, S, F, R, D), bf),
+        ],
+        in_specs=[any_, vm, vm, vm, any_],
+        out_specs=[any_, vm, vm, vm, vm, vm, any_, any_],
+        scratch_shapes=[
+            V((3 * C, D), bf),
+            V((nh, L, HD), bf),
+            V((2, T, D), bf),
+            V((2, T, D), bf),
+            V((NW, F, R, D), bf),
+            dma((2,)),
+            dma((2,)),
+            dma((2,)),
+            dma((2 * P_,)),
+            dma((2 * P_,)),
+            dma((2 * P_,)),
+            dma((2 * P_,)),
+        ],
+        compiler_params=pltpu.CompilerParams(
+            collective_id=3, has_side_effects=True, vmem_limit_bytes=60 << 20
+        ),
+        name="forward",
+    )(x_all, w, g1, sc, wz)
+
+
 def body(
     inputs,
     w_query,
@@ -533,36 +701,34 @@
     qkv_rows = jnp.stack([w_query, w_key, w_value], 1).astype(bf).reshape(shard, 3, groups, cols)
     qkv_rows = qkv_rows.transpose(2, 0, 1, 3).reshape(groups, shard, 3 * cols)
     small = jnp.stack([gain_first, gain_second, bias_up, bias_down], 0)
-    small = jnp.pad(small, ((0, 4), (0, 128 - shard)))
+    small = jnp.pad(small.astype(bf), ((0, 12), (0, 128 - shard)))
     weights = jnp.stack([w_proj, w_up, w_down], 0).astype(bf)
     x_all, qkv_w, small, weights = gather_all(groups, rows_of, x_low, qkv_rows, small, weights)
-    x_all = x_all.reshape(length, width)
-    qkv_w = qkv_w.reshape(width, 3, cols).transpose(1, 0, 2)
-    small = small[:, :, :4, :shard].transpose(2, 0, 1, 3).reshape(4, width).astype(bf).astype(f32)
+    qkv_w = qkv_w.reshape(width, 3 * cols)
+    small = small[:, :, :4, :shard].transpose(2, 0, 1, 3).reshape(4, width).astype(f32)
     first_gain, second_gain, upbias, downbias = small[0], small[1], small[2], small[3]
+    scale_dims = jax.nn.softplus(query_scale) * log_two_inverse / math.sqrt(HD)
+    scale_cols = jnp.tile(scale_dims, nh)
+    normed, qt, kt, vt, ot, lse, mixed, weights = forward_all(
+        groups, rows_of, nh, x_all, qkv_w, small[:1], scale_cols[:, None], weights
+    )
     weights = weights.reshape(3, width, width)
     proj_w, up_w, down_w = weights[0], weights[1], weights[2]
-    scale_dims = jax.nn.softplus(query_scale) * log_two_inverse / math.sqrt(HD)
-    scale_cols = jnp.tile(scale_dims, nh)
-
-    x_wide = x_all.astype(f32)
-    hat = x_wide * lax.rsqrt(jnp.mean(x_wide * x_wide, axis=-1, keepdims=True) + eps_norm)
-    normed = (hat * first_gain).astype(bf)
-    query_full = jnp.dot(normed, qkv_w[0], preferred_element_type=f32)
-    query_low = (query_full * scale_cols).astype(bf)
-    key_low = jnp.dot(normed, qkv_w[1], preferred_element_type=f32).astype(bf)
-    value_low = jnp.dot(normed, qkv_w[2], preferred_element_type=f32).astype(bf)
+    mixed = mixed.reshape(width, tokens)
+    normed = normed.reshape(length, width)
+    qkv_w = qkv_w.reshape(width, 3, cols).transpose(1, 0, 2)
+    x_all = x_all.reshape(length, width)
 
     def by_head(a):
-        return a.reshape(length, nh, HD).transpose(1, 0, 2)
+        return a.reshape(nh, HD, length)
 
     def flip(a):
         return jnp.swapaxes(a, 1, 2)
 
-    q, k, v = by_head(query_low), by_head(key_low), by_head(value_low)
-    qt, kt, vt = flip(q), flip(k), flip(v)
-    ot, lse = flash_fwd(qt, k, vt, min(1024, length), min(512, length))
-    mixed = lax.all_to_all(ot.reshape(cols, length), "seq", split_axis=1, concat_axis=0, tiled=True)
+    qt, kt, vt, ot = by_head(qt), by_head(kt), by_head(vt), by_head(ot)
+    q, k, v = flip(qt), flip(kt), flip(vt)
+    lse = lse.reshape(nh, 1, length)
+    query_full = qt.reshape(cols, length).T.astype(f32) / scale_cols
     float_in = x_low.astype(f32)
     middle = float_in + dot(mixed, proj_w, 0, 0)
     second = rms_scale(middle, second_gain).astype(bf)
@@ -605,6 +771,8 @@
     back = dot(dq, qkv_w[0], 1, 1) + dot(dk, qkv_w[1], 1, 1) + dot(dv, qkv_w[2], 1, 1)
     scale_row = jnp.pad(scale_part, (0, width - HD))
     zeros = jnp.zeros_like(scale_row)
+    wide = x_all.astype(f32)
+    hat = wide * lax.rsqrt(jnp.mean(wide * wide, axis=-1, keepdims=True) + eps_norm)
     grad_gfirst = jnp.sum(back * hat, axis=0)
     vectors = jnp.stack([grad_gfirst, grad_gsecond, grad_bup, grad_bdown, scale_row, zeros, zeros, zeros], 0)
     stacked = jnp.stack([grad_wproj.astype(bf), grad_wup.astype(bf), grad_wdown.astype(bf)], 0)

time: 598 us -> 571 us (0.955)
  matrix products: 102 us -> 87.4 us
  Pallas kernels: 345 us -> 336 us
  waiting for transfers between devices: 8.8 us -> 0.01 us
  local copies, waits for them, and re-layouts: 74.5 us -> 80.7 us
    pallas_call x1, Pallas kernels: 126 us -> 73.1 us  [gather_all(): pl.pallas_call(functools.partial(gather_kernel, S, F), out_shape=[jax.Sha...]
    pallas_call x1, Pallas kernels: 34.2 us -> 74.7 us  [forward_all(): pl.pallas_call(functools.partial(forward_kernel, S, F, nh), out_shape=[sh...]
    dot_general x3 -> x0, matrix products: 17.6 us -> none  [the longest x1 9.43 us: body(): query_full = jnp.dot(normed, qkv_w[0], preferred_element_type=f32)]
    all_to_all x1, waiting for transfers between devices: 8.8 us -> 0.01 us  [body(): lax.all_to_all(grad_mixed, 'seq', split_axis=0, concat_axis=1, tiled=True)]
    all_to_all x1, starting transfers between devices: 4.1 us -> 12.5 us  [body(): lax.all_to_all(grad_mixed, 'seq', split_axis=0, concat_axis=1, tiled=True)]
    convert_element_type x2 -> x1, other arithmetic: 7.59 us -> 0.85 us  [body(): small[:, :, :4, :shard].transpose(2, 0, 1, 3).reshape(4, width).astype(f32)]
    slice x4 -> x5, local copies, waits for them, and re-layouts: 11.3 us -> 17.5 us  [the longest x2 11.6 us: body(): qkv_w[2]]
  transfers between devices with their start and end apart: 2 -> 1, of which waited for: 1 -> 0; matrix products, arithmetic and copies ran while one was open for 6% -> 15% of each run, Pallas kernels for 0% -> 0%
where the time goes in v3:
time: 571 us; the launch traced here: 560 us
  Pallas kernels  336 us (59%)
  matrix products  87.4 us (15%)
  local copies, waits for them, and re-layouts  80.7 us (14%)
  other arithmetic  42.1 us (7%)
  starting transfers between devices  12.5 us (2%)
    pallas_call x1, Pallas kernels, scatter_all(): pl.pallas_call(functools.partial(scatter_kernel, S, F), out_shape=[jax.Sh...  127 us
    dot_general x13, matrix products, dot(): lax.dot_general(a, b, (((ca,), (cb,)), ((), ())), preferred_element_type=...  78.7 us
    pallas_call x1, Pallas kernels, forward_all(): pl.pallas_call(functools.partial(forward_kernel, S, F, nh), out_shape=[sh...  74.7 us
    pallas_call x1, Pallas kernels, gather_all(): pl.pallas_call(functools.partial(gather_kernel, S, F), out_shape=[jax.Sha...  73.1 us
    pallas_call x1, Pallas kernels, flash_bwd(): pl.pallas_call(functools.partial(bwd_kernel, BQ, BK), grid=(L // BQ,), in...  60.5 us
    dot_general x1, local copies, waits for them, and re-layouts, dot(): lax.dot_general(a, b, (((ca,), (cb,)), ((), ())), preferred_element_type=...  14.4 us
    all_to_all x1, starting transfers between devices, body(): lax.all_to_all(grad_mixed, 'seq', split_axis=0, concat_axis=1, tiled=True)  12.5 us
    slice x2, local copies, waits for them, and re-layouts, body(): qkv_w[2]  11.6 us
  transfers between devices with their start and end apart: 1, of which 0 were waited for; matrix products, arithmetic and copies ran while one was open for 15% of the time, Pallas kernels for 0%

profile of v3, /device:TPU:0, one launch (start us, length us, event | category | flops | bytes accessed | tf_op | source)
XLA Modules:
  0.0 560.0 jit_solution(1569081149568053333)
XLA Ops:
  11.2 73.1 %gather.1 = (bf16[8,512,1280]{2,1,0:T(8,128)(2,1)}, bf16[8,4,40,480]{3,2,1,0:T(8,128)(2,1)}, bf16[8,4,16,128]{3,2,1,0:T(8,128)(2,1)}, bf16[3,4,40,1280]{3,2,1,0:T(8,128)(2,1)}) custom-call(bf16[512,1280]{1,0:T(8,128)(2,1)} %bitcast.163, bf16[8,40,480]{2,1,0:T(8,128)(2,1)} %reshape.211.wq, bf16[16,128]{1,0:T(8,128)(2,1)} %fusion.33.sm, ...), custom_call_target="tpu_custom_call" | custom-call | tf_op jit(solution)/shard_map/gather/pallas_call | solution.py:199
  86.2 74.7 %forward.1 = (bf16[8,512,1280]{2,1,0:T(8,128)(2,1)}, bf16[160,4096]{1,0:T(8,128)(2,1)}, bf16[160,4096]{1,0:T(8,128)(2,1)}, bf16[160,4096]{1,0:T(8,128)(2,1)}, bf...) custom-call(bf16[8,512,1280]{2,1,0:T(8,128)(2,1)} %get-tuple-element, ...), custom_call_target="tpu_custom_call" | custom-call | tf_op jit(solution)/shard_map/forward/pallas_call | solution.py:642
  160.9 4.5 fusion.41
  178.4 12.5 %all-to-all-start = ((bf16[8,160,512]{2,1,0:T(8,128)(2,1)}), bf16[8,160,512]{2,1,0:T(8,128)(2,1)}, u32[]{:S(2)}, u32[]{:S(2)}) async-start(bf16[8,160,512]{2,1,0:T(8,128)(2,1)} %bitcast.27), calls=%async_computation | async-start | bytes 2621440 | tf_op jit(solution)/shard_map/all_to_all | solution.py:756
  191.0 6.2 %multiply_reduce_fusion = f32[8,512]{1,0:T(8,128)S(1)} fusion(bf16[8,512,1280]{2,1,0:T(8,128)(2,1)} %get-tuple-element.32.x_all), kind=kLoop, calls=%fused_computation.3 | loop fusion | flops 15724544 | bytes 10502144 | tf_op jit(solution)/shard_map/reduce_sum | solution.py:775
  200.5 6.0 %convolution_convert_fusion.1 = bf16[1280,1280]{1,0:T(8,128)(2,1)} fusion(bf16[512,1280]{1,0:T(8,128)(2,1)} %copy-done.30, f32[512,1280]{1,0:T(8,128)} %copy-done.4, f32[1280]{0:T(1024)S(1)} %mul.163, f32[512]{0:T(512)S(1)} %fusion.37), kind=kOutput, calls=%fused_computation.7 | convolution fusion | flops 1681326080 | bytes 7216128 | tf_op jit(solution)/shard_map/dot_general | solution.py:25
  206.5 3.7 convolution_convert_fusion
  210.2 3.6 convolution_convert_fusion.2
  214.1 8.0 %fusion.42 = (bf16[1,1280,160]{2,0,1:T(2,128)(2,1)}, bf16[1,1280,160]{2,0,1:T(2,128)(2,1)}, bf16[1,1280,160]{2,0,1:T(2,128)(2,1)S(1)}) fusion(bf16[3,1280,160]{2,0,1:T(4,128)(2,1)} %bitcast.164), kind=kLoop, calls=%fused_computation.105 | loop fusion | bytes 2457600 | tf_op jit(solution)/shard_map/slice | solution.py:771
  222.1 3.6 copy.100
  231.5 3.8 copy.92
  235.3 3.7 copy.93
  241.7 6.8 %fusion.5 = bf16[1,512,1280]{2,1,0:T(8,128)(2,1)} fusion(f32[512,1280]{1,0:T(8,128)} %copy-done.4, bf16[1280,1280]{1,0:T(8,128)(2,1)} %bitcast.191, f32[1280]{0:T(1024)S(1)} %add.104, f32[512,1280]{1,0:T(8,128)} %copy-done.28), kind=kOutput, calls=%fused_computation.24 | convolution fusion | flops 1682964480 | bytes 9835520 | tf_op jit(solution)/shard_map/dot_general | solution.py:737
  248.5 14.4 %copy.101 = bf16[1280,4096]{1,0:T(8,128)(2,1)} copy(bf16[1280,4096]{0,1:T(8,128)(2,1)} %bitcast.167) | data formatting | bytes 20971520 | tf_op jit(solution)/shard_map/dot_general | solution.py:25
  262.8 9.5 %pad_maximum_fusion.g = bf16[3,8,4,40,1280]{4,3,2,1,0:T(8,128)(2,1)} fusion(bf16[1,8,4,40,1280]{4,3,2,1,0:T(8,128)(2,1)} %bitcast.193, bf16[1,8,4,40,1280]{4,3,2,1,0:T(8,128)(2,1)} %bitcast.192, bf16[1,8,4,40,1280]{4,3,2,1,0:T(8,128)(2,1)} %bitcast.194), kind=kLoop, calls=%fused_computation.5 | loop fusion | flops 9830400 | bytes 19660800 | tf_op jit(solution)/shard_map/stack | solution.py:778
  282.6 60.5 %bwd512_512.1 = (bf16[2,80,4096]{2,1,0:T(8,128)(2,1)}, bf16[2,4096,80]{2,1,0:T(8,128)(2,1)}, bf16[2,4096,80]{2,1,0:T(8,128)(2,1)}) custom-call(bf16[2,80,4096]{2,1,0:T(8,128)(2,1)} %bitcast.165, bf16[2,4096,80]{2,1,0:T(8,128)(2,1)} %bitcast.178, bf16[2,80,4096]{2,1,0:T(8,128)(2,1)} %bitcast.185, bf16[2,4096,80]{2,1,0:T(8,128)(2,1)} %bitcast.176, ...), custom_call_target="tpu_custom_call" | custom-call | tf_op jit(solution)/shard_map/bwd512_512/pallas_call | solution.py:61
  347.7 3.9 copy.97
  351.6 4.0 copy.99
  358.0 7.4 %convolution_convert_fusion.4 = bf16[8,4,40,160]{3,2,1,0:T(8,128)(2,1)S(1)} fusion(bf16[8,4,40,4096]{3,2,1,0:T(8,128)(2,1)} %bitcast.168, bf16[4096,160,1,1]{0,1,3,2:T(8,128)(2,1)} %bitcast.174), kind=kOutput, calls=%fused_computation.40 | convolution fusion | flops 1677926400 | bytes 12206080 | tf_op jit(solution)/shard_map/dot_general | solution.py:25
  365.5 7.2 %convolution_convert_fusion.5 = bf16[8,4,40,160]{3,2,1,0:T(8,128)(2,1)S(1)} fusion(bf16[8,4,40,4096]{3,2,1,0:T(8,128)(2,1)} %bitcast.169, bf16[4096,160,1,1]{0,1,3,2:T(8,128)(2,1)S(1)} %bitcast.180), kind=kOutput, calls=%fused_computation.41 | convolution fusion | flops 1677926400 | bytes 12206080 | tf_op jit(solution)/shard_map/dot_general | solution.py:25
  376.0 8.6 %fusion.23 = f32[4096,1280]{1,0:T(8,128)} fusion(bf16[4096,160]{0,1:T(8,128)(2,1)S(1)} %bitcast.183, bf16[1,1280,160]{1,2,0:T(8,128)(2,1)S(1)} %copy-done.16), kind=kOutput, calls=%fused_computation.56 | convolution fusion | flops 1677721600 | bytes 22691840 | tf_op jit(solution)/shard_map/dot_general | solution.py:25
  384.6 10.5 %fusion.21 = f32[4096,1280]{1,0:T(8,128)} fusion(bf16[4096,160]{0,1:T(8,128)(2,1)S(1)} %bitcast.181, bf16[1,1280,160]{1,2,0:T(8,128)(2,1)S(1)} %copy.98), kind=kOutput, calls=%fused_computation.54 | convolution fusion | flops 1677721600 | bytes 22691840 | tf_op jit(solution)/shard_map/dot_general | solution.py:25
  395.1 18.7 %fusion.1 = (f32[1280]{0:T(1024)S(1)}, bf16[4096,1280]{1,0:T(8,128)(2,1)}) fusion(f32[4096]{0:T(1024)S(1)} %bitcast.201, bf16[8,512,1280]{2,1,0:T(8,128)(2,1)S(1)} %bitcast.159, bf16[4096,160]{0,1:T(8,128)(2,1)S(1)} %bitcast.175, bf16[1,1280,160]{1,2,0:T(8,128)(2,1)S(1)} %copy-done.17, f32[4096,1280]{1,0:T(8,128)} %fusion.23, f32[4096,1280]{1,0:T(8,128)} %fusion.21), kind=kOutput, calls=%fused_computation.2 | convolution fusion | flops 1714420480 | bytes 64656384 | tf_op jit(solution)/shard_map/dot_general | solution.py:25
  416.4 127.3 %scatter.1 = (f32[3,40,1280]{2,1,0:T(8,128)}, f32[512,1280]{1,0:T(8,128)}, bf16[8,40,480]{2,1,0:T(8,128)(2,1)}, f32[8,1280]{1,0:T(8,128)}) custom-call(bf16[3,8,4,40,1280]{4,3,2,1,0:T(8,128)(2,1)} %pad_maximum_fusion.g, bf16[8,512,1280]{2,1,0:T(8,128)(2,1)} %bitcast.160, bf16[8,4,40,480]{3,2,1,0:T(8,128)(2,1)} %pad_maximum_fusion.1.q, f32[8,1280]{1,0:T(8,128)} %stack.101.vec), custom_call_target="tpu_custom_call" | custom-call | tf_op jit(solution)/shard_map/scatter/pallas_call | solution.py:420
  (156 shorter events, 76.0 us)
Async XLA Ops:
  4.2 5.5 copy-start.23
  4.2 5.5 copy-start.24
  4.3 5.5 copy-start.25
  4.3 5.5 copy-start.20
  4.3 5.5 copy-start.21
  167.6 6.9 %copy-start.4 = (f32[512,1280]{1,0:T(8,128)}, f32[512,1280]{1,0:T(8,128)S(1)}, u32[]{:S(2)}) copy-start(f32[512,1280]{1,0:T(8,128)S(1)} %get-tuple-element.83) | copy-start | bytes 7864324
  178.4 93.9 %all-to-all-start = ((bf16[8,160,512]{2,1,0:T(8,128)(2,1)}), bf16[8,160,512]{2,1,0:T(8,128)(2,1)}, u32[]{:S(2)}, u32[]{:S(2)}) async-start(bf16[8,160,512]{2,1,0:T(8,128)(2,1)} %bitcast.27), calls=%async_computation | async-start | bytes 2621440 | tf_op jit(solution)/shard_map/all_to_all | solution.py:756
  191.0 6.2 %copy-start.11 = (bf16[8,4,40,480]{3,2,1,0:T(8,128)(2,1)S(1)}, bf16[8,4,40,480]{3,2,1,0:T(8,128)(2,1)}, u32[]{:S(2)}) copy-start(bf16[8,4,40,480]{3,2,1,0:T(8,128)(2,1)} %get-tuple-element.33) | copy-start | bytes 3686404
  200.5 6.0 %copy-start.19 = (bf16[1,512,1280]{2,1,0:T(8,128)(2,1)S(1)}, bf16[1,512,1280]{2,1,0:T(8,128)(2,1)}, u32[]{:S(2)}) copy-start(bf16[1,512,1280]{2,1,0:T(8,128)(2,1)} %param.25) | copy-start | bytes 3932164
  200.5 6.0 %copy-start.29 = (f32[512,1280]{1,0:T(8,128)S(1)}, f32[512,1280]{1,0:T(8,128)}, u32[]{:S(2)}) copy-start(f32[512,1280]{1,0:T(8,128)} %copy-done.28) | copy-start | bytes 7864324
  222.1 8.8 %copy-start.22 = (f32[2,4096]{1,0:T(2,128)S(1)}, f32[2,4096]{1,0:T(2,128)}, u32[]{:S(2)}) copy-start(f32[2,4096]{1,0:T(2,128)} %get-tuple-element.41) | copy-start | bytes 98308
  231.5 7.6 %copy-start.2 = (bf16[160,4096]{1,0:T(8,128)(2,1)S(1)}, bf16[160,4096]{1,0:T(8,128)(2,1)}, u32[]{:S(2)}) copy-start(bf16[160,4096]{1,0:T(8,128)(2,1)} %get-tuple-element.38) | copy-start | bytes 3932164
  347.7 7.9 %copy-start.3 = (bf16[160,4096]{1,0:T(8,128)(2,1)S(1)}, bf16[160,4096]{1,0:T(8,128)(2,1)}, u32[]{:S(2)}) copy-start(bf16[160,4096]{1,0:T(8,128)(2,1)} %get-tuple-element.38) | copy-start | bytes 3932164
  358.0 7.5 %copy-start.9 = (bf16[4096,2,80]{0,2,1:T(8,128)(2,1)S(1)}, bf16[4096,2,80]{0,2,1:T(8,128)(2,1)}, u32[]{:S(2)}) copy-start(bf16[4096,2,80]{0,2,1:T(8,128)(2,1)} %copy.97) | copy-start | bytes 3932164
  358.0 14.7 %slice-start.3 = ((s8[10485760]{0:T(1024)(128)(4,1)}), s8[4194304]{0:T(1024)(128)(4,1)S(1)}, s32[]{:S(2)}) async-start(s8[10485760]{0:T(1024)(128)(4,1)} %bitcast.170), calls=%async_computation.4 | async-start | bytes 8388608
  358.0 14.7 %slice-start.4 = ((s8[10485760]{0:T(1024)(128)(4,1)}), s8[4194304]{0:T(1024)(128)(4,1)S(1)}, s32[]{:S(2)}) async-start(s8[10485760]{0:T(1024)(128)(4,1)} %bitcast.170), calls=%async_computation.5 | async-start | bytes 8388608
  365.5 7.2 %slice-start.5 = ((s8[10485760]{0:T(1024)(128)(4,1)}), s8[2097152]{0:T(1024)(128)(4,1)S(1)}, s32[]{:S(2)}) async-start(s8[10485760]{0:T(1024)(128)(4,1)} %bitcast.170), calls=%async_computation.6 | async-start | bytes 4194304
  365.5 7.2 %copy-start.10 = (bf16[2,80,4096]{2,1,0:T(8,128)(2,1)S(1)}, bf16[2,80,4096]{2,1,0:T(8,128)(2,1)}, u32[]{:S(2)}) copy-start(bf16[2,80,4096]{2,1,0:T(8,128)(2,1)} %multiply_convert_fusion) | copy-start | bytes 3932164
  384.6 10.5 %slice-start = ((s8[10485760]{0:T(1024)(128)(4,1)}), s8[4194304]{0:T(1024)(128)(4,1)S(1)}, s32[]{:S(2)}) async-start(s8[10485760]{0:T(1024)(128)(4,1)} %bitcast.158), calls=%async_computation.1 | async-start | bytes 8388608
  384.6 10.5 %slice-start.1 = ((s8[10485760]{0:T(1024)(128)(4,1)}), s8[4194304]{0:T(1024)(128)(4,1)S(1)}, s32[]{:S(2)}) async-start(s8[10485760]{0:T(1024)(128)(4,1)} %bitcast.158), calls=%async_computation.2 | async-start | bytes 8388608
  384.6 10.5 %slice-start.2 = ((s8[10485760]{0:T(1024)(128)(4,1)}), s8[2097152]{0:T(1024)(128)(4,1)S(1)}, s32[]{:S(2)}) async-start(s8[10485760]{0:T(1024)(128)(4,1)} %bitcast.158), calls=%async_computation.3 | async-start | bytes 4194304
  384.6 10.5 %copy-start.8 = (bf16[4096,2,80]{0,2,1:T(8,128)(2,1)S(1)}, bf16[4096,2,80]{0,2,1:T(8,128)(2,1)}, u32[]{:S(2)}) copy-start(bf16[4096,2,80]{0,2,1:T(8,128)(2,1)} %copy.99) | copy-start | bytes 3932164
  384.6 10.5 %copy-start.17 = (bf16[1,1280,160]{1,2,0:T(8,128)(2,1)S(1)}, bf16[1,1280,160]{1,2,0:T(8,128)(2,1)}, u32[]{:S(2)}) copy-start(bf16[1,1280,160]{1,2,0:T(8,128)(2,1)} %copy.100) | copy-start | bytes 1228804
  416.4 127.3 %copy-start.27 = (f32[80]{0:T(128)S(1)}, f32[80]{0:T(128)}, u32[]{:S(2)}) copy-start(f32[80]{0:T(128)} %param.24) | copy-start | bytes 964
  (14 other events, 49.2 us)
